TPU v7x, 32 devices: a whole 2x2x4 slice. The times are simulated.
32 devices in a mesh: dp: 8 (over z, x), tensor: 4 (over y, core).
Axes of the slice: x: 2, y: 2, z: 4, core: 2. Of those that a mesh axis runs over, the one named last changes fastest.
Arguments:
- x_in: bfloat16 [20480, 768], P(('dp', 'tensor')), may hold values from -6 to 6
- tags: int32 [128], P('dp'), may hold values from 0 to 1, as said below
- lengths: int32 [128], P('dp'), may hold values from 95 to 160, as said below
- w_qkv: bfloat16 [2, 768, 3, 768], P(None, 'dp', None, 'tensor'), may hold values from -0.3125 to 0.3125
- w_out: bfloat16 [2, 768, 768], P(None, 'dp', 'tensor'), may hold values from -1.5 to 1.5
- w_up: bfloat16 [2, 768, 3072], P(None, 'dp', 'tensor'), may hold values from -0.21875 to 0.21875
- w_down: bfloat16 [2, 768, 3072], P(None, 'dp', 'tensor'), may hold values from -0.109375 to 0.109375
- norm_gain: float32 [2, 2, 768], P(None, None, ('dp', 'tensor')), may hold values from 0.5 to 1.5
- norm_bias: float32 [2, 2, 768], P(None, None, ('dp', 'tensor')), may hold values from -2 to 2
- cotangent: bfloat16 [20480, 768], P(('dp', 'tensor')), may hold values from -6 to 6
Outputs:
- y_out: bfloat16 [20480, 768], P(('dp', 'tensor'))
- x_grad: float32 [20480, 768], P(('dp', 'tensor'))
- qkv_grad: float32 [2, 768, 3, 768], P(None, 'dp', None, 'tensor')
- out_grad: float32 [2, 768, 768], P(None, 'dp', 'tensor')
- up_grad: float32 [2, 768, 3072], P(None, 'dp', 'tensor')
- down_grad: float32 [2, 768, 3072], P(None, 'dp', 'tensor')
- gain_grad: float32 [2, 2, 768], P(None, None, ('dp', 'tensor'))
- bias_grad: float32 [2, 2, 768], P(None, None, ('dp', 'tensor'))
Inputs may be any that keep to these rules, and one draw needn't show every extreme that they name: `tags`: within the chains of each index of dp (a block of 16 in order), all heavy chains (0) come before all light ones (1); each block holds at least a quarter of either type. `lengths`: each device's chains (blocks of 4 in order) include one of length 160.
All inputs are finite; a program needn't handle non-finite values.
Results may differ from a plain program's by a relative error of at most 0.02.
Values may be sent and summed in bfloat16 or wider, within the bound.
A program may use at most 192 MiB of HBM per device.

v0:
```python
from functools import partial

import jax
import jax.numpy as jnp
from jax import lax
from jax.sharding import PartitionSpec as P

D = 768
HEAD_DIM = 64
LENGTH = 160
MICRO = 4
CHAINS_PART = 1


EPS = 1e-12
NEG = -1e30
HIGH = lax.Precision.HIGHEST


def typed_map(operand, stacked, chain_kinds, pattern):

    def single(element):
        weight = lax.dynamic_index_in_dim(stacked, element[1], 0, keepdims=False)
        return jnp.einsum(pattern, element[0], weight, preferred_element_type=jnp.float32)

    return lax.map(single, (operand, chain_kinds))


def typed_grads(running, operand, partner, chain_kinds, pattern):

    def single(carry, element):
        product_term = jnp.einsum(
            pattern, element[0], element[1], preferred_element_type=jnp.float32
        )
        previous = lax.dynamic_index_in_dim(carry, element[2], 0, keepdims=False)
        return (
            lax.dynamic_update_index_in_dim(carry, previous + product_term, element[2], 0),
            None,
        )

    return lax.scan(single, running, (operand, partner, chain_kinds))[0]


def row_terms(operand, stacked, chain_kinds, pattern, row_count):
    result = typed_map(operand, stacked, chain_kinds, pattern)
    return result.reshape(row_count, result.shape[-1])


def norm_forward(values, gain_rows, shift_rows):
    center = values - jnp.mean(values, -1, keepdims=True)
    factor = lax.rsqrt(jnp.mean(center * center, -1, keepdims=True) + EPS)
    normed = center * factor
    return (normed * gain_rows + shift_rows, normed, factor)


def norm_backward(grad_out, normed, factor, gain_rows):
    scaled = grad_out * gain_rows
    mean_plain = jnp.mean(scaled, -1, keepdims=True)
    mean_normed = jnp.mean(scaled * normed, -1, keepdims=True)
    return factor * (scaled - mean_plain - normed * mean_normed)


def type_sums(onehot, values):
    return jnp.dot(onehot.T, values, precision=HIGH, preferred_element_type=jnp.float32)


def local(x_in, tags, lengths, w_qkv, w_out, w_up, w_down, norm_gain, norm_bias, cotangent):
    tp_count = lax.axis_size("tensor")
    tp_index = lax.axis_index("tensor")
    local_rows = CHAINS_PART * LENGTH
    batch_chains = tp_count * CHAINS_PART
    head_cols = w_qkv.shape[3]
    local_heads = head_cols // HEAD_DIM
    tag_grid = tags.reshape(tp_count, MICRO, CHAINS_PART)
    len_grid = lengths.reshape(tp_count, MICRO, CHAINS_PART)
    own_tags = lax.dynamic_index_in_dim(tag_grid, tp_index, 0, keepdims=False)
    gains, shifts = (
        lax.all_gather(norm_gain, ("dp", "tensor"), axis=2, tiled=True),
        lax.all_gather(norm_bias, ("dp", "tensor"), axis=2, tiled=True),
    )
    grad_full = (
        jnp.zeros((2, D, 3, head_cols), jnp.float32),
        jnp.zeros((2, D, head_cols), jnp.float32),
        jnp.zeros((2, D, w_up.shape[2]), jnp.float32),
        jnp.zeros((2, D, w_down.shape[2]), jnp.float32),
    )
    shards = (
        jnp.zeros(w_qkv.shape, jnp.float32),
        jnp.zeros(w_out.shape, jnp.float32),
        jnp.zeros(w_up.shape, jnp.float32),
        jnp.zeros(w_down.shape, jnp.float32),
    )
    gain_acc = jnp.zeros((2, 2, D), jnp.float32)
    shift_acc = jnp.zeros((2, 2, D), jnp.float32)
    outputs = []
    input_grads = []
    for micro_index in range(MICRO):
        held = (
            lax.all_gather(w_qkv, "dp", axis=1, tiled=True),
            lax.all_gather(w_out, "dp", axis=1, tiled=True),
            lax.all_gather(w_up, "dp", axis=1, tiled=True),
            lax.all_gather(w_down, "dp", axis=1, tiled=True),
        )
        qkv_w, out_w, up_w, down_w = held
        chain_kinds = tag_grid[:, micro_index].reshape(batch_chains)
        chain_lens = len_grid[:, micro_index].reshape(batch_chains)
        own_rows = x_in[micro_index * local_rows : (micro_index + 1) * local_rows]
        kinds_rows = jnp.repeat(own_tags[micro_index], LENGTH)
        heavy_rows = (kinds_rows == 0)[:, None]
        onehot = (kinds_rows[:, None] == jnp.arange(2)[None, :]).astype(jnp.float32)
        gain_mid = jnp.where(heavy_rows, gains[0, 0], gains[1, 0])
        shift_mid = jnp.where(heavy_rows, shifts[0, 0], shifts[1, 0])
        gain_end = jnp.where(heavy_rows, gains[0, 1], gains[1, 1])
        shift_end = jnp.where(heavy_rows, shifts[0, 1], shifts[1, 1])
        gathered = lax.all_gather(own_rows, "tensor", axis=0, tiled=True).reshape(
            batch_chains, LENGTH, D
        )
        projected = typed_map(gathered, qkv_w, chain_kinds, "ld,dkh->lkh").astype(jnp.bfloat16)
        query = projected[:, :, 0].reshape(batch_chains, LENGTH, local_heads, HEAD_DIM)
        keys_low = projected[:, :, 1].reshape(batch_chains, LENGTH, local_heads, HEAD_DIM)
        values_low = projected[:, :, 2].reshape(batch_chains, LENGTH, local_heads, HEAD_DIM)
        valid = (
            lax.broadcasted_iota(jnp.int32, (batch_chains, 1, 1, LENGTH), 3)
            < chain_lens[:, None, None, None]
        )
        scores = (
            jnp.einsum("cqhe,ckhe->chqk", query, keys_low, preferred_element_type=jnp.float32)
            * 0.125
        )
        scores = jnp.where(valid, scores, NEG)
        highest = jnp.max(scores, -1, keepdims=True)
        expo = jnp.exp(scores - highest)
        totals = jnp.sum(expo, -1, keepdims=True)
        probs = expo / totals
        log_total = highest + jnp.log(totals)
        heads_low = jnp.einsum(
            "chqk,ckhe->cqhe",
            probs.astype(jnp.bfloat16),
            values_low,
            preferred_element_type=jnp.float32,
        ).astype(jnp.bfloat16)
        heads_low = heads_low.reshape(batch_chains, LENGTH, head_cols)
        attn_sum = lax.psum_scatter(
            row_terms(
                heads_low, out_w, chain_kinds, "lh,dh->ld", lax.axis_size("tensor") * local_rows
            ).astype(jnp.bfloat16),
            "tensor",
            scatter_dimension=0,
            tiled=True,
        ).astype(jnp.float32)
        mid, normed_mid, factor_mid = norm_forward(
            own_rows.astype(jnp.float32) + attn_sum, gain_mid, shift_mid
        )
        mid_all = lax.all_gather(mid.astype(jnp.bfloat16), "tensor", axis=0, tiled=True).reshape(
            batch_chains, LENGTH, D
        )
        up_value = typed_map(mid_all, up_w, chain_kinds, "ld,df->lf")
        act_low = jax.nn.gelu(up_value, approximate=False).astype(jnp.bfloat16)
        ffn_sum = lax.psum_scatter(
            row_terms(
                act_low, down_w, chain_kinds, "lf,df->ld", lax.axis_size("tensor") * local_rows
            ).astype(jnp.bfloat16),
            "tensor",
            scatter_dimension=0,
            tiled=True,
        ).astype(jnp.float32)
        final, normed_end, factor_end = norm_forward(ffn_sum + mid, gain_end, shift_end)
        outputs.append(final.astype(jnp.bfloat16))
        base = grad_full
        grad_final = cotangent[micro_index * local_rows : (micro_index + 1) * local_rows].astype(
            jnp.float32
        )
        gain_acc = gain_acc.at[:, 1].add(type_sums(onehot, grad_final * normed_end))
        shift_acc = shift_acc.at[:, 1].add(type_sums(onehot, grad_final))
        grad_resid2 = norm_backward(grad_final, normed_end, factor_end, gain_end)
        grad_ffn = lax.all_gather(
            grad_resid2.astype(jnp.bfloat16), "tensor", axis=0, tiled=True
        ).reshape(batch_chains, LENGTH, D)
        grad_act = typed_map(grad_ffn, down_w, chain_kinds, "ld,df->lf")
        unused_value, gelu_back = jax.vjp(partial(jax.nn.gelu, approximate=False), up_value)
        grad_up = gelu_back(grad_act)[0].astype(jnp.bfloat16)
        down_acc = typed_grads(base[3], grad_ffn, act_low, chain_kinds, "ld,lf->df")
        up_acc = typed_grads(base[2], mid_all, grad_up, chain_kinds, "ld,lf->df")
        grad_mid = grad_resid2 + lax.psum_scatter(
            row_terms(
                grad_up, up_w, chain_kinds, "lf,df->ld", lax.axis_size("tensor") * local_rows
            ).astype(jnp.bfloat16),
            "tensor",
            scatter_dimension=0,
            tiled=True,
        ).astype(jnp.float32)
        gain_acc = gain_acc.at[:, 0].add(type_sums(onehot, grad_mid * normed_mid))
        shift_acc = shift_acc.at[:, 0].add(type_sums(onehot, grad_mid))
        grad_resid1 = norm_backward(grad_mid, normed_mid, factor_mid, gain_mid)
        grad_attn = lax.all_gather(
            grad_resid1.astype(jnp.bfloat16), "tensor", axis=0, tiled=True
        ).reshape(batch_chains, LENGTH, D)
        grad_heads = typed_map(grad_attn, out_w, chain_kinds, "ld,dh->lh").astype(jnp.bfloat16)
        out_acc = typed_grads(base[1], grad_attn, heads_low, chain_kinds, "ld,lh->dh")
        grad_heads = grad_heads.reshape(batch_chains, LENGTH, local_heads, HEAD_DIM)
        again = (
            jnp.einsum("cqhe,ckhe->chqk", query, keys_low, preferred_element_type=jnp.float32)
            * 0.125
        )
        probs_again = jnp.exp(jnp.where(valid, again, NEG) - log_total)
        grad_probs = jnp.einsum(
            "cqhe,ckhe->chqk", grad_heads, values_low, preferred_element_type=jnp.float32
        )
        inner = jnp.sum(grad_probs * probs_again, -1, keepdims=True)
        grad_scores = (probs_again * (grad_probs - inner)).astype(jnp.bfloat16)
        grad_query = (
            jnp.einsum("chqk,ckhe->cqhe", grad_scores, keys_low, preferred_element_type=jnp.float32)
            * 0.125
        ).astype(jnp.bfloat16)
        grad_keys = (
            jnp.einsum("chqk,cqhe->ckhe", grad_scores, query, preferred_element_type=jnp.float32)
            * 0.125
        ).astype(jnp.bfloat16)
        grad_values = jnp.einsum(
            "chqk,cqhe->ckhe",
            probs_again.astype(jnp.bfloat16),
            grad_heads,
            preferred_element_type=jnp.float32,
        ).astype(jnp.bfloat16)
        grad_proj = jnp.stack([grad_query, grad_keys, grad_values], 2).reshape(
            batch_chains, LENGTH, 3, head_cols
        )
        qkv_acc = typed_grads(base[0], gathered, grad_proj, chain_kinds, "ld,lkh->dkh")
        grad_input = grad_resid1 + lax.psum_scatter(
            row_terms(
                grad_proj, qkv_w, chain_kinds, "lkh,dkh->ld", lax.axis_size("tensor") * local_rows
            ).astype(jnp.bfloat16),
            "tensor",
            scatter_dimension=0,
            tiled=True,
        ).astype(jnp.float32)
        input_grads.append(grad_input)
        updated = (qkv_acc, out_acc, up_acc, down_acc)
        grad_full = updated
    shards = (
        lax.psum_scatter(grad_full[0], "dp", scatter_dimension=1, tiled=True),
        lax.psum_scatter(grad_full[1], "dp", scatter_dimension=1, tiled=True),
        lax.psum_scatter(grad_full[2], "dp", scatter_dimension=1, tiled=True),
        lax.psum_scatter(grad_full[3], "dp", scatter_dimension=1, tiled=True),
    )
    gain_grad, shift_grad = (
        lax.psum_scatter(gain_acc, ("dp", "tensor"), scatter_dimension=2, tiled=True),
        lax.psum_scatter(shift_acc, ("dp", "tensor"), scatter_dimension=2, tiled=True),
    )
    return (
        jnp.concatenate(outputs, 0),
        jnp.concatenate(input_grads, 0),
        shards[0],
        shards[1],
        shards[2],
        shards[3],
        gain_grad,
        shift_grad,
    )


def solution(mesh):
    placed = (
        P(("dp", "tensor"), None),
        P("dp"),
        P("dp"),
        P(None, "dp", None, "tensor"),
        P(None, "dp", "tensor"),
        P(None, "dp", "tensor"),
        P(None, "dp", "tensor"),
        P(None, None, ("dp", "tensor")),
        P(None, None, ("dp", "tensor")),
        P(("dp", "tensor"), None),
    )
    return jax.shard_map(
        local,
        mesh=mesh,
        in_specs=placed,
        out_specs=(
            P(("dp", "tensor"), None),
            P(("dp", "tensor"), None),
            P(None, "dp", None, "tensor"),
            P(None, "dp", "tensor"),
            P(None, "dp", "tensor"),
            P(None, "dp", "tensor"),
            P(None, None, ("dp", "tensor")),
            P(None, None, ("dp", "tensor")),
        ),
        check_vma=False,
    )
```

profile of v0, /device:TPU:5, one launch (start us, length us, event | category | flops | bytes accessed | tf_op | source)
XLA Modules:
  0.0 1805.5 jit_solution(13706230249261995386)
XLA Ops:
  14.6 29.1 %all_gather.80 = bf16[2,768,192]{2,1,0:T(8,128)(2,1)S(1)} all-gather(bf16[2,96,192]{2,1,0:T(8,128)(2,1)S(1)} %copy-done.112), channel_id=1, replica_groups=mesh['dp'=8,'tensor'=4] {'dp'}, dimensions={1}, use_global_device_ids=true | all-gather | bytes 663552 | tf_op jit(solution)/shard_map/all_gather | solution.py:100
  127.8 21.1 %while.508 = (s32[]{:T(128)}, bf16[4,160,3,192]{3,1,2,0:T(8,128)(2,1)}, bf16[4,160,768]{2,1,0:T(8,128)(2,1)}, s32[4]{0:T(128)}, bf16[2,768,3,192]{1,3,2,0:T(8,128)(2,1)S(1)}, /*index=5*/s32[]{:T(128)}, s32[]{:T(128)}, s32[]{:T(128)}) while((s32[]{:T(128)}, bf16[4,160,3,192]{3,1,2,0:T(8,128)(2,1)}, bf16[4,160,768]{2,1,0:T(8,128)(2,1)}, ...), condition=%wide.region_49.50_spmd, body=%wide.region_48.49_spmd.sunk | while | flops 141557760 | bytes 1623175 | solution.py:26
  184.1 41.9 %all_gather.81 = f32[2,2,768]{1,0,2:T(2,128)S(1)} all-gather(f32[2,2,24]{1,0,2:T(2,128)S(1)} %copy.210), channel_id=1, replica_groups=mesh['dp'=8,'tensor'=4] {'dp','tensor'}, dimensions={2}, use_global_device_ids=true | all-gather | bytes 12672 | tf_op jit(solution)/shard_map/all_gather | solution.py:78
  226.2 44.2 %all_gather.82 = f32[2,2,768]{1,0,2:T(2,128)S(1)} all-gather(f32[2,2,24]{1,0,2:T(2,128)S(1)} %copy.211), channel_id=1, replica_groups=mesh['dp'=8,'tensor'=4] {'dp','tensor'}, dimensions={2}, use_global_device_ids=true | all-gather | bytes 12672 | tf_op jit(solution)/shard_map/all_gather | solution.py:79
  422.3 21.3 %while.499 = (s32[]{:T(128)}, bf16[4,160,768]{2,1,0:T(8,128)(2,1)}, bf16[4,160,768]{2,1,0:T(8,128)(2,1)}, s32[4]{0:T(128)S(1)}, bf16[2,768,768]{2,1,0:T(8,128)(2,1)}, /*index=5*/s32[]{:T(128)}, s32[]{:T(128)}, s32[]{:T(128)}) while((s32[]{:T(128)}, bf16[4,160,768]{2,1,0:T(8,128)(2,1)}, bf16[4,160,768]{2,1,0:T(8,128)(2,1)}, ...), condition=%wide.region_12.13_spmd, body=%wide.region_11.12_spmd.sunk | while | flops 188743680 | bytes 1918087 | solution.py:26
  962.7 22.8 %while.520 = (s32[]{:T(128)}, f32[4,160,768]{2,1,0:T(8,128)}, bf16[4,160,768]{2,1,0:T(8,128)(2,1)}, s32[4]{0:T(128)}, bf16[2,768,768]{2,1,0:T(8,128)(2,1)}, /*index=5*/s32[]{:T(128)}, s32[]{:T(128)}, s32[]{:T(128)}) while((s32[]{:T(128)}, f32[4,160,768]{2,1,0:T(8,128)}, bf16[4,160,768]{2,1,0:T(8,128)(2,1)}, s32[4]{0:T(128)}, ...), condition=%wide.region_97.98_spmd, body=%wide.region_96.97_spmd.sunk | while | flops 188743680 | bytes 1918087 | solution.py:26
  1014.8 23.1 %while.532 = (s32[]{:T(128)}, f32[2,768,192]{1,2,0:T(8,128)}, s32[4]{0:T(128)S(1)}, bf16[4,160,768]{2,1,0:T(8,128)(2,1)}, bf16[4,160,192]{2,1,0:T(8,128)(2,1)}, /*index=5*/s32[]{:T(128)}, s32[]{:T(128)}, s32[]{:T(128)}) while((s32[]{:T(128)}, f32[2,768,192]{1,2,0:T(8,128)}, s32[4]{0:T(128)S(1)}, bf16[4,160,768]{2,1,0:T(8,128)(2,1)}, ...), condition=%wide.region_134.135_spmd, body=%wide.region_133.134_spmd.sunk | while | flops 47333380 | bytes 2688139 | solution.py:41
  1058.9 30.3 %while.528 = (s32[]{:T(128)}, f32[2,768,3,192]{1,3,2,0:T(8,128)}, s32[4]{0:T(128)}, bf16[4,160,768]{2,1,0:T(8,128)(2,1)}, bf16[4,160,3,192]{3,1,2,0:T(8,128)(2,1)}, /*index=5*/s32[]{:T(128)}, s32[]{:T(128)}, s32[]{:T(128)}) while((s32[]{:T(128)}, f32[2,768,3,192]{1,3,2,0:T(8,128)}, s32[4]{0:T(128)}, bf16[4,160,768]{2,1,0:T(8,128)(2,1)}, ...), condition=%wide.region_125.126_spmd, body=%wide.region_124.125_spmd.sunk | while | flops 142000128 | bytes 7570571 | solution.py:41
  1273.7 23.1 %while.533 = (s32[]{:T(128)}, f32[2,768,192]{1,2,0:T(8,128)}, s32[4]{0:T(128)S(1)}, bf16[4,160,768]{2,1,0:T(8,128)(2,1)}, bf16[4,160,192]{2,1,0:T(8,128)(2,1)}, /*index=5*/s32[]{:T(128)}, s32[]{:T(128)}, s32[]{:T(128)}) while((s32[]{:T(128)}, f32[2,768,192]{1,2,0:T(8,128)}, s32[4]{0:T(128)S(1)}, bf16[4,160,768]{2,1,0:T(8,128)(2,1)}, ...), condition=%wide.region_136.137_spmd, body=%wide.region_135.136_spmd.sunk | while | flops 47333380 | bytes 2688139 | solution.py:41
  1317.5 23.1 %while.534 = (s32[]{:T(128)}, f32[2,768,192]{1,2,0:T(8,128)}, s32[4]{0:T(128)S(1)}, bf16[4,160,768]{2,1,0:T(8,128)(2,1)}, bf16[4,160,192]{2,1,0:T(8,128)(2,1)}, /*index=5*/s32[]{:T(128)}, s32[]{:T(128)}, s32[]{:T(128)}) while((s32[]{:T(128)}, f32[2,768,192]{1,2,0:T(8,128)}, s32[4]{0:T(128)S(1)}, bf16[4,160,768]{2,1,0:T(8,128)(2,1)}, ...), condition=%wide.region_138.139_spmd, body=%wide.region_137.138_spmd.sunk | while | flops 47333380 | bytes 2688139 | solution.py:41
  1340.7 22.7 %while.535 = (s32[]{:T(128)}, f32[2,768,192]{1,2,0:T(8,128)}, s32[4]{0:T(128)S(1)}, bf16[4,160,768]{2,1,0:T(8,128)(2,1)S(1)}, bf16[4,160,192]{2,1,0:T(8,128)(2,1)}, /*index=5*/s32[]{:T(128)}, s32[]{:T(128)}, s32[]{:T(128)}) while((s32[]{:T(128)}, f32[2,768,192]{1,2,0:T(8,128)}, s32[4]{0:T(128)S(1)}, ...), condition=%wide.region_140.141_spmd, body=%wide.region_139.140_spmd.sunk | while | flops 47333380 | bytes 2688139 | solution.py:41
  1366.2 27.8 %while.529 = (s32[]{:T(128)}, f32[2,768,3,192]{1,3,2,0:T(8,128)}, s32[4]{0:T(128)S(1)}, bf16[4,160,768]{2,1,0:T(8,128)(2,1)}, bf16[4,160,3,192]{3,1,2,0:T(8,128)(2,1)}, /*index=5*/s32[]{:T(128)}, s32[]{:T(128)}, s32[]{:T(128)}) while((s32[]{:T(128)}, f32[2,768,3,192]{1,3,2,0:T(8,128)}, s32[4]{0:T(128)S(1)}, ...), condition=%wide.region_127.128_spmd, body=%wide.region_126.127_spmd.sunk | while | flops 142000128 | bytes 7570571 | solution.py:41
  1394.1 27.9 %while.530 = (s32[]{:T(128)}, f32[2,768,3,192]{1,3,2,0:T(8,128)}, s32[4]{0:T(128)S(1)}, bf16[4,160,768]{2,1,0:T(8,128)(2,1)}, bf16[4,160,3,192]{3,1,2,0:T(8,128)(2,1)}, /*index=5*/s32[]{:T(128)}, s32[]{:T(128)}, s32[]{:T(128)}) while((s32[]{:T(128)}, f32[2,768,3,192]{1,3,2,0:T(8,128)}, s32[4]{0:T(128)S(1)}, ...), condition=%wide.region_129.130_spmd, body=%wide.region_128.129_spmd.sunk | while | flops 142000128 | bytes 7570571 | solution.py:41
  1422.0 27.9 %while.531 = (s32[]{:T(128)}, f32[2,768,3,192]{1,3,2,0:T(8,128)}, s32[4]{0:T(128)S(1)}, bf16[4,160,768]{2,1,0:T(8,128)(2,1)}, bf16[4,160,3,192]{3,1,2,0:T(8,128)(2,1)}, /*index=5*/s32[]{:T(128)}, s32[]{:T(128)}, s32[]{:T(128)}) while((s32[]{:T(128)}, f32[2,768,3,192]{1,3,2,0:T(8,128)}, s32[4]{0:T(128)S(1)}, ...), condition=%wide.region_131.132_spmd, body=%wide.region_130.131_spmd.sunk | while | flops 142000128 | bytes 7570571 | solution.py:41
  1458.3 29.9 %while.540 = (s32[]{:T(128)}, f32[2,768,768]{2,1,0:T(8,128)}, s32[4]{0:T(128)S(1)}, bf16[4,160,768]{2,1,0:T(8,128)(2,1)}, bf16[4,160,768]{2,1,0:T(8,128)(2,1)}, /*index=5*/s32[]{:T(128)}, s32[]{:T(128)}, s32[]{:T(128)}) while((s32[]{:T(128)}, f32[2,768,768]{2,1,0:T(8,128)}, s32[4]{0:T(128)S(1)}, bf16[4,160,768]{2,1,0:T(8,128)(2,1)}, ...), condition=%wide.region_152.153_spmd, body=%wide.region_151.152_spmd.sunk | while | flops 189333504 | bytes 9929867 | solution.py:41
  1488.2 29.9 %while.541 = (s32[]{:T(128)}, f32[2,768,768]{2,1,0:T(8,128)}, s32[4]{0:T(128)S(1)}, bf16[4,160,768]{2,1,0:T(8,128)(2,1)}, bf16[4,160,768]{2,1,0:T(8,128)(2,1)}, /*index=5*/s32[]{:T(128)}, s32[]{:T(128)}, s32[]{:T(128)}) while((s32[]{:T(128)}, f32[2,768,768]{2,1,0:T(8,128)}, s32[4]{0:T(128)S(1)}, bf16[4,160,768]{2,1,0:T(8,128)(2,1)}, ...), condition=%wide.region_154.155_spmd, body=%wide.region_153.154_spmd.sunk | while | flops 189333504 | bytes 9929867 | solution.py:41
  1518.1 29.9 %while.542 = (s32[]{:T(128)}, f32[2,768,768]{2,1,0:T(8,128)}, s32[4]{0:T(128)S(1)}, bf16[4,160,768]{2,1,0:T(8,128)(2,1)}, bf16[4,160,768]{2,1,0:T(8,128)(2,1)}, /*index=5*/s32[]{:T(128)}, s32[]{:T(128)}, s32[]{:T(128)}) while((s32[]{:T(128)}, f32[2,768,768]{2,1,0:T(8,128)}, s32[4]{0:T(128)S(1)}, bf16[4,160,768]{2,1,0:T(8,128)(2,1)}, ...), condition=%wide.region_156.157_spmd, body=%wide.region_155.156_spmd.sunk | while | flops 189333504 | bytes 9929867 | solution.py:41
  1548.0 29.7 %while.543 = (s32[]{:T(128)}, f32[2,768,768]{2,1,0:T(8,128)}, s32[4]{0:T(128)S(1)}, bf16[4,160,768]{2,1,0:T(8,128)(2,1)}, bf16[4,160,768]{2,1,0:T(8,128)(2,1)}, /*index=5*/s32[]{:T(128)}, s32[]{:T(128)}, s32[]{:T(128)}) while((s32[]{:T(128)}, f32[2,768,768]{2,1,0:T(8,128)}, s32[4]{0:T(128)S(1)}, bf16[4,160,768]{2,1,0:T(8,128)(2,1)}, ...), condition=%wide.region_158.159_spmd, body=%wide.region_157.158_spmd.sunk | while | flops 189333504 | bytes 9929867 | solution.py:41
  1580.3 30.6 %while.536 = (s32[]{:T(128)}, f32[2,768,768]{2,1,0:T(8,128)}, s32[4]{0:T(128)S(1)}, bf16[4,160,768]{2,1,0:T(8,128)(2,1)}, bf16[4,160,768]{2,1,0:T(8,128)(2,1)}, /*index=5*/s32[]{:T(128)}, s32[]{:T(128)}, s32[]{:T(128)}) while((s32[]{:T(128)}, f32[2,768,768]{2,1,0:T(8,128)}, s32[4]{0:T(128)S(1)}, bf16[4,160,768]{2,1,0:T(8,128)(2,1)}, ...), condition=%wide.region_143.144_spmd, body=%wide.region_142.143_spmd.sunk | while | flops 189333504 | bytes 9929867 | solution.py:41
  1611.0 30.5 %while.537 = (s32[]{:T(128)}, f32[2,768,768]{2,1,0:T(8,128)}, s32[4]{0:T(128)S(1)}, bf16[4,160,768]{2,1,0:T(8,128)(2,1)}, bf16[4,160,768]{2,1,0:T(8,128)(2,1)}, /*index=5*/s32[]{:T(128)}, s32[]{:T(128)}, s32[]{:T(128)}) while((s32[]{:T(128)}, f32[2,768,768]{2,1,0:T(8,128)}, s32[4]{0:T(128)S(1)}, bf16[4,160,768]{2,1,0:T(8,128)(2,1)}, ...), condition=%wide.region_145.146_spmd, body=%wide.region_144.145_spmd.sunk | while | flops 189333504 | bytes 9929867 | solution.py:41
  1641.4 29.9 %while.538 = (s32[]{:T(128)}, f32[2,768,768]{2,1,0:T(8,128)}, s32[4]{0:T(128)S(1)}, bf16[4,160,768]{2,1,0:T(8,128)(2,1)}, bf16[4,160,768]{2,1,0:T(8,128)(2,1)}, /*index=5*/s32[]{:T(128)}, s32[]{:T(128)}, s32[]{:T(128)}) while((s32[]{:T(128)}, f32[2,768,768]{2,1,0:T(8,128)}, s32[4]{0:T(128)S(1)}, bf16[4,160,768]{2,1,0:T(8,128)(2,1)}, ...), condition=%wide.region_147.148_spmd, body=%wide.region_146.147_spmd.sunk | while | flops 189333504 | bytes 9929867 | solution.py:41
  1671.3 29.5 %while.539 = (s32[]{:T(128)}, f32[2,768,768]{2,1,0:T(8,128)}, s32[4]{0:T(128)S(1)}, bf16[4,160,768]{2,1,0:T(8,128)(2,1)}, bf16[4,160,768]{2,1,0:T(8,128)(2,1)}, /*index=5*/s32[]{:T(128)}, s32[]{:T(128)}, s32[]{:T(128)}) while((s32[]{:T(128)}, f32[2,768,768]{2,1,0:T(8,128)}, s32[4]{0:T(128)S(1)}, bf16[4,160,768]{2,1,0:T(8,128)(2,1)}, ...), condition=%wide.region_149.150_spmd, body=%wide.region_148.149_spmd.sunk | while | flops 189333504 | bytes 9929867 | solution.py:41
  1712.1 42.5 %all-reduce.2 = (f32[2,2,768]{2,0,1:T(2,128)S(1)}, f32[2,2,768]{2,0,1:T(2,128)S(1)}) all-reduce(f32[2,2,768]{2,0,1:T(2,128)S(1)} %fusion.329, f32[2,2,768]{2,0,1:T(2,128)S(1)} %fusion.335), channel_id=22, replica_groups=mesh['dp'=8,'tensor'=4] {'dp','tensor'}, use_global_device_ids=true, to_apply=%region_160.161.clone | all-reduce | flops 6144 | bytes 49152
  1761.6 36.9 %reduce-scatter.59.cloned.1.call-done = f32[2,96,768]{2,1,0:T(8,128)} async-done(((f32[2,768,768]{2,1,0:T(8,128)}), f32[2,96,768]{2,1,0:T(8,128)}) %reduce-scatter.59.cloned.1.call-update) | async-done | bytes 589840 | tf_op jit(solution)/shard_map/reduce_scatter | solution.py:243
  (1218 shorter events, 1752.3 us)
Async XLA Ops:
  7.2 61.0 %all-gather.4.cloned.1.call-start = ((), (), s32[]{:S(2)}) async-start(), calls=%async_computation.20 | async-start | bytes 2654208 | tf_op jit(solution)/shard_map/all_gather | solution.py:99
  9.2 317.8 %reduce-scatter.23.cloned.1.call-start = ((), (), s32[]{:S(2)}) async-start(), calls=%async_computation.21 | async-start | bytes 1228800 | tf_op jit(solution)/shard_map/reduce_scatter | solution.py:143
  9.3 169.8 %copy-start.3 = (bf16[4,160,768]{2,1,0:T(8,128)(2,1)}, bf16[4,160,768]{2,1,0:T(8,128)(2,1)S(1)}, u32[]{:S(2)}) copy-start(bf16[4,160,768]{2,1,0:T(8,128)(2,1)S(1)} %fusion.470) | copy-start | bytes 2949124
  126.8 201.4 %reduce-scatter.35.cloned.1.call-start = ((), (), s32[]{:S(2)}) async-start(), calls=%async_computation.29 | async-start | bytes 1228800 | tf_op jit(solution)/shard_map/reduce_scatter | solution.py:143
  175.0 166.4 %all-gather.6.cloned.1.call-start = ((), (), s32[]{:S(2)}) async-start(), calls=%async_computation.22 | async-start | bytes 2654208 | tf_op jit(solution)/shard_map/all_gather | solution.py:101
  175.6 190.9 %all-gather.8.cloned.1.call-start = ((), (), s32[]{:S(2)}) async-start(), calls=%async_computation.23 | async-start | bytes 2654208 | tf_op jit(solution)/shard_map/all_gather | solution.py:102
  176.2 369.6 %reduce-scatter.37.cloned.1.call-start = ((), (), s32[]{:S(2)}) async-start(), calls=%async_computation.30 | async-start | bytes 1228800 | tf_op jit(solution)/shard_map/reduce_scatter | solution.py:159
  385.3 160.6 %reduce-scatter.25.cloned.1.call-start = ((), (), s32[]{:S(2)}) async-start(), calls=%async_computation.24 | async-start | bytes 1228800 | tf_op jit(solution)/shard_map/reduce_scatter | solution.py:159
  443.7 222.8 %reduce-scatter.31.cloned.1.call-start = ((), (), s32[]{:S(2)}) async-start(), calls=%async_computation.27 | async-start | bytes 1228800 | tf_op jit(solution)/shard_map/reduce_scatter | solution.py:143
  492.1 174.3 %reduce-scatter.27.cloned.1.call-start = ((), (), s32[]{:S(2)}) async-start(), calls=%async_computation.25 | async-start | bytes 1228800 | tf_op jit(solution)/shard_map/reduce_scatter | solution.py:143
  545.7 120.7 %reduce-scatter.51.cloned.1.call-start = ((), (), s32[]{:S(2)}) async-start(), calls=%async_computation.37 | async-start | bytes 1228800 | tf_op jit(solution)/shard_map/reduce_scatter | solution.py:184
  606.2 78.3 %reduce-scatter.39.cloned.1.call-start = ((), (), s32[]{:S(2)}) async-start(), calls=%async_computation.31 | async-start | bytes 1228800 | tf_op jit(solution)/shard_map/reduce_scatter | solution.py:184
  664.2 106.3 %reduce-scatter.29.cloned.1.call-start = ((), (), s32[]{:S(2)}) async-start(), calls=%async_computation.26 | async-start | bytes 1228800 | tf_op jit(solution)/shard_map/reduce_scatter | solution.py:159
  746.4 108.8 %reduce-scatter.33.cloned.1.call-start = ((), (), s32[]{:S(2)}) async-start(), calls=%async_computation.28 | async-start | bytes 1228800 | tf_op jit(solution)/shard_map/reduce_scatter | solution.py:159
  831.2 258.2 %reduce-scatter.43.cloned.1.call-start = ((), (), s32[]{:S(2)}) async-start(), calls=%async_computation.33 | async-start | bytes 1228800 | tf_op jit(solution)/shard_map/reduce_scatter | solution.py:184
  950.8 138.6 %reduce-scatter.47.cloned.1.call-start = ((), (), s32[]{:S(2)}) async-start(), calls=%async_computation.35 | async-start | bytes 1228800 | tf_op jit(solution)/shard_map/reduce_scatter | solution.py:184
  1038.4 717.6 %reduce-scatter.41.cloned.1.call-start = ((), (), s32[]{:S(2)}) async-start(), calls=%async_computation.32 | async-start | bytes 1228800 | tf_op jit(solution)/shard_map/reduce_scatter | solution.py:229
  1089.3 667.6 %reduce-scatter.45.cloned.1.call-start = ((), (), s32[]{:S(2)}) async-start(), calls=%async_computation.34 | async-start | bytes 1228800 | tf_op jit(solution)/shard_map/reduce_scatter | solution.py:229
  1253.2 505.0 %reduce-scatter.49.cloned.1.call-start = ((), (), s32[]{:S(2)}) async-start(), calls=%async_computation.36 | async-start | bytes 1228800 | tf_op jit(solution)/shard_map/reduce_scatter | solution.py:229
  1296.8 462.4 %reduce-scatter.53.cloned.1.call-start = ((), (), s32[]{:S(2)}) async-start(), calls=%async_computation.38 | async-start | bytes 1228800 | tf_op jit(solution)/shard_map/reduce_scatter | solution.py:229
  1340.6 421.0 %reduce-scatter.57.cloned.1.call-start = ((), (), s32[]{:S(2)}) async-start(), calls=%async_computation.40 | async-start | bytes 1769472 | tf_op jit(solution)/shard_map/reduce_scatter | solution.py:242
  1394.1 367.5 %reduce-scatter.55.cloned.1.call-start = ((), (), s32[]{:S(2)}) async-start(), calls=%async_computation.39 | async-start | bytes 5308416 | tf_op jit(solution)/shard_map/reduce_scatter | solution.py:241
  1455.5 306.1 %reduce-scatter.61.cloned.1.call-start = ((), (), s32[]{:S(2)}) async-start(), calls=%async_computation.42 | async-start | bytes 5308416 | tf_op jit(solution)/shard_map/reduce_scatter | solution.py:244
  1577.8 220.7 %reduce-scatter.59.cloned.1.call-start = ((), (), s32[]{:S(2)}) async-start(), calls=%async_computation.41 | async-start | bytes 5308416 | tf_op jit(solution)/shard_map/reduce_scatter | solution.py:243
  (217 other events, 2170.2 us)
Sparse Core Ops, SparseCore 0:
  10.8 56.0 all-gather.3
  126.9 24.6 reduce-scatter.22
  175.1 26.5 reduce-scatter.34
  203.7 53.1 all-gather.5
  259.0 51.3 all-gather.7
  385.4 20.3 reduce-scatter.36
  443.8 20.2 reduce-scatter.24
  492.3 20.2 reduce-scatter.30
  545.8 20.3 reduce-scatter.26
  606.3 20.2 reduce-scatter.50
  664.3 20.1 reduce-scatter.38
  746.5 23.8 reduce-scatter.28
  831.3 23.8 reduce-scatter.32
  950.9 23.9 reduce-scatter.42
  1038.0 23.8 reduce-scatter.46
  1089.4 23.9 reduce-scatter.40
  1253.3 23.9 reduce-scatter.44
  1296.9 23.9 reduce-scatter.48
  1340.7 23.9 reduce-scatter.52
  1394.2 64.1 reduce-scatter.56
  1463.0 95.4 reduce-scatter.54
  1577.9 96.2 reduce-scatter.60
  1701.1 97.4 reduce-scatter.58
where the time goes:
time: 1830 us; the launch traced here: 1810 us
  matrix products  479 us (26%)
  local copies, waits for them, and re-layouts  380 us (21%)
  loops' own time  376 us (21%)
  blocking collectives  327 us (18%)
  other arithmetic  137 us (7%)
  waiting for transfers between devices  85.6 us (5%)
  between operations  19.6 us (1%)
    dot_general x128, matrix products, single(): jnp.einsum(pattern, element[0], weight, preferred_element_type=jnp.float32)  256 us
    another operation x32, loops' own time, typed_map(): return lax.map(single, (operand, chain_kinds))  250 us
    dot_general x64, matrix products, single(): jnp.einsum(pattern, element[0], element[1], preferred_element_type=jnp.fl...  177 us
    dynamic_slice x192, local copies, waits for them, and re-layouts, typed_map(): return lax.map(single, (operand, chain_kinds))  137 us
    another operation x16, loops' own time, typed_grads(): return lax.scan(single, running, (operand, partner, chain_kinds))[0]  126 us
    dynamic_slice x64, local copies, waits for them, and re-layouts, single(): previous = lax.dynamic_index_in_dim(carry, element[2], 0, keepdims=False)  103 us
    all_gather x4, blocking collectives, local(): lax.all_gather(own_rows, 'tensor', axis=0, tiled=True)  44.9 us
    all_gather x1, blocking collectives, local(): lax.all_gather(norm_bias, ('dp', 'tensor'), axis=2, tiled=True)  44.2 us
  transfers between devices with their start and end apart: 23, of which 4 were waited for; matrix products, arithmetic and copies ran while one was open for 45% of the time, Pallas kernels for 0%

commit v1 on v0

--- a/solution.py
+++ b/solution.py
@@ -3,18 +3,449 @@
 import jax
 import jax.numpy as jnp
 from jax import lax
+from jax.experimental import pallas as pl
+from jax.experimental.pallas import tpu as pltpu
+from jax.sharding import Mesh
 from jax.sharding import PartitionSpec as P
 
 D = 768
+HEADS = 12
 HEAD_DIM = 64
-LENGTH = 160
 MICRO = 4
 CHAINS_PART = 1
-
+LENGTH = 160
+GROUPS = 4
+OWN = 4
+EXTRA = 2
+SLOTS = OWN + EXTRA
+EXT_ROWS = EXTRA * LENGTH
+OWN_ROWS = OWN * LENGTH
+ROWS = SLOTS * LENGTH
 
 EPS = 1e-12
 NEG = -1e30
 HIGH = lax.Precision.HIGHEST
+BF = jnp.bfloat16
+F32 = jnp.float32
+MESH = pl.DeviceIdType.MESH
+ANY = pl.BlockSpec(memory_space=pl.ANY)
+AXES = ("z", "x", "y", "c")
+
+
+def place():
+    return tuple(lax.axis_index(a) for a in AXES)
+
+
+def meet(nz, z, x, y, c):
+    barrier = pltpu.get_barrier_semaphore()
+    friends = [{"c": 1 - c}, {"y": 1 - y}, {"y": 1 - y, "c": 1 - c}, {"x": 1 - x}]
+    friends += [{"z": lax.rem(z + dz, nz)} for dz in range(1, nz)]
+    for friend in friends:
+        pl.semaphore_signal(barrier, inc=1, device_id=friend, device_id_type=MESH)
+    pl.semaphore_wait(barrier, len(friends))
+
+
+def gather_kernel(nz, rows, x_in, cot, qo, up, dn, norms, w, x_ext, cot_ext, n_all,
+                  y_s, y_r, z_s, z_r, x_s, x_r, c_s, c_r, e_s, e_r, n_s, n_r, l_s):
+    z, x, y, c = place()
+    mats = (qo, up, dn)
+
+    def block(m, t, zz, xx):
+        off = pl.multiple_of((zz * 2 + xx) * rows, rows)
+        return w.at[m, t, pl.ds(off, rows)]
+
+    def send(src, dst, s_sem, r_sem, who):
+        return pltpu.make_async_remote_copy(
+            src_ref=src, dst_ref=dst, send_sem=s_sem, recv_sem=r_sem, device_id=who, device_id_type=MESH
+        )
+
+    meet(nz, z, x, y, c)
+    sent = []
+
+    def go(copy):
+        copy.start()
+        sent.append(copy)
+
+    groups = (2 * y + c, 2 * (1 - y) + c)
+    locals_ = []
+    for m in range(3):
+        go(send(mats[m].at[1 - y], block(m, groups[0], z, x), y_s.at[m], y_r.at[m], {"y": 1 - y}))
+    me = ((z * 2 + x) * 2 + y) * 2 + c
+    copy = pltpu.make_async_copy(norms, n_all.at[me], l_s.at[3])
+    copy.start()
+    for m in range(3):
+        cp = pltpu.make_async_copy(mats[m].at[y], block(m, groups[0], z, x), l_s.at[m])
+        cp.start()
+        locals_.append(cp)
+
+    @pl.when(y != c)
+    def _():
+        for i, arr in enumerate((x_in, cot)):
+            out = (x_ext, cot_ext)[i]
+            for j, (who, part) in enumerate((({"y": 1 - y}, c), ({"y": 1 - y, "c": 1 - c}, 1 - c))):
+                src = arr.at[pl.ds(pl.multiple_of(part * EXT_ROWS, EXT_ROWS), EXT_ROWS)]
+                send(src, out, e_s.at[i, j], e_r.at[i], who).start()
+
+    def spread(m, g, src):
+        t = groups[g]
+        for dz in range(1, nz):
+            go(send(src, block(m, t, z, x), z_s.at[m, g, dz], z_r.at[m, g, dz], {"z": lax.rem(z + dz, nz)}))
+        go(send(src, block(m, t, z, x), x_s.at[m, g, 0], x_r.at[m, g, 0], {"x": 1 - x}))
+        go(send(src, block(m, t, z, x), c_s.at[m, g, 0, 0], c_r.at[m, g, 0, 0], {"c": 1 - c}))
+
+    def arrived(m, g, dz, xx, sem):
+        zz = lax.rem(z + nz - dz, nz)
+        ref = block(m, groups[g], zz, xx)
+        send(ref, ref, sem, sem, {"c": 1 - c}).wait_recv()
+        return ref
+
+    for m in range(3):
+        spread(m, 0, mats[m].at[y])
+    copy.wait()
+    n1 = send(n_all.at[me], n_all.at[me], n_s.at[0], n_r.at[0], {"c": 1 - c})
+    go(n1)
+    n1.wait_recv()
+    base = pl.multiple_of(me - c, 2)
+    n2 = send(n_all.at[pl.ds(base, 2)], n_all.at[pl.ds(base, 2)], n_s.at[1], n_r.at[1], {"y": 1 - y})
+    go(n2)
+    n2.wait_recv()
+    base = pl.multiple_of((z * 2 + x) * 4, 4)
+    n3 = send(n_all.at[pl.ds(base, 4)], n_all.at[pl.ds(base, 4)], n_s.at[2], n_r.at[2], {"x": 1 - x})
+    go(n3)
+    n3.wait_recv()
+    base = pl.multiple_of(z * 8, 8)
+    for dz in range(1, nz):
+        go(send(n_all.at[pl.ds(base, 8)], n_all.at[pl.ds(base, 8)], n_s.at[2 + dz], n_r.at[2 + dz], {"z": lax.rem(z + dz, nz)}))
+    for m in range(3):
+        ref = block(m, groups[1], z, x)
+        send(ref, ref, y_r.at[m], y_r.at[m], {"y": 1 - y}).wait_recv()
+        spread(m, 1, ref)
+    for m in range(3):
+        for g in range(2):
+            for dz in range(1, nz):
+                ref = arrived(m, g, dz, x, z_r.at[m, g, dz])
+                go(send(ref, ref, x_s.at[m, g, dz], x_r.at[m, g, dz], {"x": 1 - x}))
+                go(send(ref, ref, c_s.at[m, g, dz, 0], c_r.at[m, g, dz, 0], {"c": 1 - c}))
+        for g in range(2):
+            for dz in range(nz):
+                ref = arrived(m, g, dz, 1 - x, x_r.at[m, g, dz])
+                go(send(ref, ref, c_s.at[m, g, dz, 1], c_r.at[m, g, dz, 1], {"c": 1 - c}))
+    for m in range(3):
+        for g in range(2):
+            for dz in range(nz):
+                zz = lax.rem(z + nz - dz, nz)
+                for q, xx in enumerate((x, 1 - x)):
+                    ref = block(m, (1 - 2 * c) + groups[g], zz, xx)
+                    send(ref, ref, c_r.at[m, g, dz, q], c_r.at[m, g, dz, q], {"c": 1 - c}).wait_recv()
+    for dz in range(1, nz):
+        zz = lax.rem(z + nz - dz, nz)
+        ref = n_all.at[pl.ds(pl.multiple_of(zz * 8, 8), 8)]
+        send(ref, ref, n_r.at[2 + dz], n_r.at[2 + dz], {"x": 1 - x}).wait_recv()
+    for i, out in enumerate((x_ext, cot_ext)):
+        send(out, out, e_r.at[i], e_r.at[i], {"y": 1 - y}).wait_recv()
+    for cp in locals_:
+        cp.wait()
+    for cp in sent:
+        cp.wait_send()
+
+    @pl.when(y != c)
+    def _():
+        for i in range(2):
+            for j in range(2):
+                src = x_in.at[pl.ds(0, EXT_ROWS)]
+                send(src, src, e_s.at[i, j], e_r.at[i], {"y": 1 - y}).wait_send()
+
+
+def gather_all(nz, x_in, cot, qo, up, dn, norms):
+    rows = qo.shape[1]
+    sem = pltpu.SemaphoreType.DMA
+    return pl.pallas_call(
+        partial(gather_kernel, nz, rows),
+        out_shape=(
+            jax.ShapeDtypeStruct((3, GROUPS, D, D), BF),
+            jax.ShapeDtypeStruct((EXT_ROWS, D), BF),
+            jax.ShapeDtypeStruct((EXT_ROWS, D), BF),
+            jax.ShapeDtypeStruct((nz * 8, 8, 128), F32),
+        ),
+        in_specs=[ANY] * 6,
+        out_specs=(ANY,) * 4,
+        scratch_shapes=[
+            sem((3,)), sem((3,)),
+            sem((3, 2, nz)), sem((3, 2, nz)),
+            sem((3, 2, nz)), sem((3, 2, nz)),
+            sem((3, 2, nz, 2)), sem((3, 2, nz, 2)),
+            sem((2, 2)), sem((2,)),
+            sem((nz + 2,)), sem((nz + 2,)),
+            sem((4,)),
+        ],
+        compiler_params=pltpu.CompilerParams(collective_id=0, has_side_effects=True),
+        name="gather_weights",
+    )(x_in, cot, qo, up, dn, norms)
+
+
+def scatter_kernel(nz, rows, grads, ngrad, y_ext, g_ext, own_out, oth_out, n_out, y_back, g_back,
+                   own, r_c, r_x, r_z, half, nbuf, n_c, n_x, n_z, nsum,
+                   c_s, c_r, x_s, x_r, z_s, z_r, y_s, y_r, e_s, e_r, n_s, n_r, l_s):
+    z, x, y, c = place()
+
+    def send(src, dst, s_sem, r_sem, who):
+        return pltpu.make_async_remote_copy(
+            src_ref=src, dst_ref=dst, send_sem=s_sem, recv_sem=r_sem, device_id=who, device_id_type=MESH
+        )
+
+    def part(zz, xx):
+        return pl.ds(pl.multiple_of((zz * 2 + xx) * rows, rows), rows)
+
+    meet(nz, z, x, y, c)
+    sent = []
+
+    def go(copy):
+        copy.start()
+        sent.append(copy)
+
+    order = [(m, g) for m in (2, 1, 0) for g in range(2)]
+    loads = {}
+    for m, g in order:
+        go(send(grads.at[m, 2 * g + 1 - c], r_c.at[m, g], c_s.at[m, g], c_r.at[m, g], {"c": 1 - c}))
+        loads[m, g] = pltpu.make_async_copy(grads.at[m, 2 * g + c], own.at[m, g], l_s.at[m, g])
+        loads[m, g].start()
+
+    for i, (src, dst) in enumerate(((y_ext, y_back), (g_ext, g_back))):
+        dst = dst.at[pl.ds(pl.multiple_of(c * EXT_ROWS, EXT_ROWS), EXT_ROWS)]
+
+        @pl.when(c == y)
+        def _():
+            send(src, dst, e_s.at[i], e_r.at[i, c], {"y": 1 - y}).start()
+
+        @pl.when(c != y)
+        def _():
+            send(src, dst, e_s.at[i], e_r.at[i, c], {"y": 1 - y, "c": 1 - c}).start()
+
+    nbuf[...] = ngrad[...]
+    a = send(nbuf, n_c, n_s.at[0], n_r.at[0], {"c": 1 - c})
+    go(a)
+    a.wait_recv()
+    nsum[0] = nbuf[...] + n_c[...]
+    b = send(nsum.at[0], n_x, n_s.at[1], n_r.at[1], {"x": 1 - x})
+    go(b)
+    b.wait_recv()
+    nsum[1] = nsum[0] + n_x[...]
+    for dz in range(1, nz):
+        go(send(nsum.at[1], n_z.at[dz], n_s.at[1 + dz], n_r.at[1 + dz], {"z": lax.rem(z + dz, nz)}))
+
+    for m, g in order:
+        loads[m, g].wait()
+        send(r_c.at[m, g], r_c.at[m, g], c_r.at[m, g], c_r.at[m, g], {"c": 1 - c}).wait_recv()
+
+        def add(zz, _):
+            for xx in (1 - x, x):
+                p = part(zz, xx)
+                own[m, g, p] = (own[m, g, p].astype(F32) + r_c[m, g, p].astype(F32)).astype(BF)
+            return 0
+
+        lax.fori_loop(0, nz, add, 0)
+        for zz in range(nz):
+            go(send(own.at[m, g, part(zz, 1 - x)], r_x.at[m, g, zz], x_s.at[m, g, zz], x_r.at[m, g, zz], {"x": 1 - x}))
+    for m, g in order:
+        for dz in range(1, nz + 1):
+            zz = lax.rem(z + dz, nz)
+            send(r_x.at[m, g, zz], r_x.at[m, g, zz], x_r.at[m, g, zz], x_r.at[m, g, zz], {"x": 1 - x}).wait_recv()
+            p = part(zz, x)
+            own[m, g, p] = (own[m, g, p].astype(F32) + r_x[m, g, zz].astype(F32)).astype(BF)
+            if dz < nz:
+                go(send(own.at[m, g, p], r_z.at[m, g, dz], z_s.at[m, g, dz], z_r.at[m, g, dz], {"z": zz}))
+    total = nsum[1]
+    for dz in range(1, nz):
+        send(n_z.at[dz], n_z.at[dz], n_r.at[1 + dz], n_r.at[1 + dz], {"x": 1 - x}).wait_recv()
+        total = total + n_z[dz]
+    n_out[y] = total
+    nd = send(n_out.at[y], n_out.at[y], n_s.at[nz + 1], n_r.at[nz + 1], {"y": 1 - y})
+    go(nd)
+    for m, g in order:
+        p = part(z, x)
+        total = own[m, g, p].astype(F32)
+        for dz in range(1, nz):
+            send(r_z.at[m, g, dz], r_z.at[m, g, dz], z_r.at[m, g, dz], z_r.at[m, g, dz], {"x": 1 - x}).wait_recv()
+            total = total + r_z[m, g, dz].astype(F32)
+
+        @pl.when(y == g)
+        def _():
+            own_out[m] = total
+
+        @pl.when(y != g)
+        def _():
+            half[m] = total.astype(BF)
+            send(half.at[m], oth_out.at[m], y_s.at[m], y_r.at[m], {"y": 1 - y}).start()
+    for m in range(3):
+        send(half.at[m], oth_out.at[m], y_s.at[m], y_r.at[m], {"y": 1 - y}).wait()
+    nd.wait_recv()
+
+    @pl.when(y != c)
+    def _():
+        for i, dst in enumerate((y_back, g_back)):
+            for j in range(2):
+                ref = dst.at[pl.ds(j * EXT_ROWS, EXT_ROWS)]
+                send(ref, ref, e_s.at[i], e_r.at[i, j], {"y": 1 - y}).wait_recv()
+
+    for i in range(2):
+        send(y_ext, y_ext, e_s.at[i], e_s.at[i], {"y": 1 - y}).wait_send()
+    for cp in sent:
+        cp.wait_send()
+
+
+def scatter_all(nz, rows, grads, ngrad, y_ext, g_ext):
+    sem = pltpu.SemaphoreType.DMA
+    V = pl.BlockSpec(memory_space=pltpu.VMEM)
+    return pl.pallas_call(
+        partial(scatter_kernel, nz, rows),
+        out_shape=(
+            jax.ShapeDtypeStruct((3, rows, D), F32),
+            jax.ShapeDtypeStruct((3, rows, D), BF),
+            jax.ShapeDtypeStruct((2, 8, D), F32),
+            jax.ShapeDtypeStruct((OWN_ROWS, D), BF),
+            jax.ShapeDtypeStruct((OWN_ROWS, D), BF),
+        ),
+        in_specs=[ANY, V, ANY, ANY],
+        out_specs=(V, ANY, V, ANY, ANY),
+        scratch_shapes=[
+            pltpu.VMEM((3, 2, D, D), BF),
+            pltpu.VMEM((3, 2, D, D), BF),
+            pltpu.VMEM((3, 2, nz, rows, D), BF),
+            pltpu.VMEM((3, 2, nz, rows, D), BF),
+            pltpu.VMEM((3, rows, D), BF),
+            pltpu.VMEM((8, D), F32),
+            pltpu.VMEM((8, D), F32),
+            pltpu.VMEM((8, D), F32),
+            pltpu.VMEM((nz, 8, D), F32),
+            pltpu.VMEM((2, 8, D), F32),
+            sem((3, 2)), sem((3, 2)),
+            sem((3, 2, nz)), sem((3, 2, nz)),
+            sem((3, 2, nz)), sem((3, 2, nz)),
+            sem((3,)), sem((3,)),
+            sem((2,)), sem((2, 2)),
+            sem((nz + 2,)), sem((nz + 2,)),
+            sem((3, 2)),
+        ],
+        compiler_params=pltpu.CompilerParams(
+            collective_id=1, has_side_effects=True, vmem_limit_bytes=48 * 1024 * 1024
+        ),
+        name="scatter_grads",
+    )(grads, ngrad, y_ext, g_ext)
+
+
+def norm_forward(values, gain, shift):
+    center = values - jnp.mean(values, -1, keepdims=True)
+    factor = lax.rsqrt(jnp.mean(center * center, -1, keepdims=True) + EPS)
+    normed = center * factor
+    return normed * gain + shift, normed, factor
+
+
+def norm_backward(grad_out, normed, factor, gain):
+    scaled = grad_out * gain
+    mean_plain = jnp.mean(scaled, -1, keepdims=True)
+    mean_normed = jnp.mean(scaled * normed, -1, keepdims=True)
+    return factor * (scaled - mean_plain - normed * mean_normed)
+
+
+def ein(pattern, *operands):
+    return jnp.einsum(pattern, *operands, preferred_element_type=F32)
+
+
+def layer(x, cot, lens, w, gains, shifts):
+    heads = HEADS // GROUPS
+    qkv_w = w[0][:, :, : 3 * heads * HEAD_DIM]
+    out_w = w[0][:, :, 3 * heads * HEAD_DIM :]
+    up_w, down_w = w[1], w[2]
+    proj = ein("nd,tdk->tnk", x, qkv_w).astype(BF)
+    parts = proj.reshape(GROUPS, SLOTS, LENGTH, 3, heads, HEAD_DIM)
+    query, key, value = parts[:, :, :, 0], parts[:, :, :, 1], parts[:, :, :, 2]
+    valid = lax.broadcasted_iota(jnp.int32, (SLOTS, LENGTH), 1) < lens[:, None]
+    scores = ein("tcqhe,tckhe->tchqk", query, key) * 0.125
+    scores = jnp.where(valid[None, :, None, None, :], scores, NEG)
+    probs = jax.nn.softmax(scores, axis=-1)
+    low = probs.astype(BF)
+    hout = ein("tchqk,tckhe->tcqhe", low, value).astype(BF).reshape(GROUPS, ROWS, heads * HEAD_DIM)
+    attn = ein("tnh,tdh->nd", hout, out_w)
+    mid, n1, s1 = norm_forward(x.astype(F32) + attn, gains[0], shifts[0])
+    mid_low = mid.astype(BF)
+    up = ein("nd,tdf->tnf", mid_low, up_w)
+    act, pull = jax.vjp(partial(jax.nn.gelu, approximate=False), up)
+    act = act.astype(BF)
+    ffn = ein("tnf,tdf->nd", act, down_w)
+    final, n2, s2 = norm_forward(ffn + mid, gains[1], shifts[1])
+    y = final.astype(BF)
+    dr2 = norm_backward(cot, n2, s2, gains[1])
+    ngrad = [None, jnp.sum(cot * n2, 0), None, jnp.sum(cot, 0)]
+    d_ffn = dr2.astype(BF)
+    d_act = ein("nd,tdf->tnf", d_ffn, down_w)
+    d_up = pull(d_act)[0].astype(BF)
+    g_down = ein("nd,tnf->tdf", d_ffn, act)
+    g_up = ein("nd,tnf->tdf", mid_low, d_up)
+    d_mid = dr2 + ein("tnf,tdf->nd", d_up, up_w)
+    dr1 = norm_backward(d_mid, n1, s1, gains[0])
+    ngrad[0] = jnp.sum(d_mid * n1, 0)
+    ngrad[2] = jnp.sum(d_mid, 0)
+    d_attn = dr1.astype(BF)
+    d_heads = ein("nd,tdh->tnh", d_attn, out_w).astype(BF)
+    g_out = ein("nd,tnh->tdh", d_attn, hout)
+    d_heads = d_heads.reshape(GROUPS, SLOTS, LENGTH, heads, HEAD_DIM)
+    d_probs = ein("tcqhe,tckhe->tchqk", d_heads, value)
+    d_scores = (probs * (d_probs - jnp.sum(d_probs * probs, -1, keepdims=True))).astype(BF)
+    d_q = (ein("tchqk,tckhe->tcqhe", d_scores, key) * 0.125).astype(BF)
+    d_k = (ein("tchqk,tcqhe->tckhe", d_scores, query) * 0.125).astype(BF)
+    d_v = ein("tchqk,tcqhe->tckhe", low, d_heads).astype(BF)
+    d_proj = jnp.stack([d_q, d_k, d_v], 3).reshape(GROUPS, ROWS, 3 * heads * HEAD_DIM)
+    g_qkv = ein("nd,tnk->tdk", x, d_proj)
+    x_grad = dr1 + ein("tnk,tdk->nd", d_proj, qkv_w)
+    grads = jnp.stack([jnp.concatenate([g_qkv, g_out], -1), g_up, g_down]).astype(BF)
+    ngrad = jnp.pad(jnp.stack(ngrad), ((0, 4), (0, 0)))
+    return y, x_grad, grads, ngrad
+
+
+def split_local(nz, x_in, tags, lengths, w_qkv, w_out, w_up, w_down, norm_gain, norm_bias, cotangent):
+    z, x, y, c = place()
+    rows = w_up.shape[1]
+    cols = norm_gain.shape[2]
+    own = 2 * y + c
+    qo = jnp.concatenate([w_qkv.reshape(2, rows, -1), w_out], -1)
+    norms = jnp.concatenate([norm_gain.reshape(4, cols), norm_bias.reshape(4, cols)], 0)
+    norms = jnp.pad(norms, ((0, 0), (0, 128 - cols)))
+    w, x_ext, cot_ext, n_all = gather_all(nz, x_in, cotangent, qo, w_up, w_down, norms)
+    params = n_all[:, :, :cols].transpose(1, 0, 2).reshape(2, 2, 2, D)
+    params = lax.dynamic_index_in_dim(params, y, 1, keepdims=False)
+
+    def slots(values):
+        mine = lax.dynamic_slice_in_dim(values, own * OWN, OWN)
+        lent = lax.dynamic_slice_in_dim(values, (2 - y) * OWN + c * EXTRA, EXTRA)
+        return jnp.concatenate([mine, lent])
+
+    kinds = slots(tags)
+    lens = slots(lengths)
+    mine = jnp.repeat(kinds == y, LENGTH)[:, None]
+    rows_x = jnp.concatenate([x_in, x_ext])
+    rows_cot = jnp.concatenate([cotangent, cot_ext]).astype(F32)
+    rows_cot = jnp.where(mine, rows_cot, 0.0)
+    y_rows, g_rows, grads, ngrad = layer(rows_x, rows_cot, lens, w, params[0], params[1])
+    own_g, oth_g, n_sum, y_back, g_back = scatter_all(
+        nz, rows, grads, ngrad, y_rows[OWN_ROWS:], g_rows[OWN_ROWS:].astype(BF)
+    )
+    y_out = jnp.where(mine[:OWN_ROWS], y_rows[:OWN_ROWS], y_back)
+    x_grad = jnp.where(mine[:OWN_ROWS], g_rows[:OWN_ROWS], g_back.astype(F32))
+    oth_g = oth_g.astype(F32)
+    both = jnp.stack([jnp.where(y == 0, own_g, oth_g), jnp.where(y == 0, oth_g, own_g)])
+    width = w_qkv.shape[2] * w_qkv.shape[3]
+    me = ((z * 2 + x) * 2 + y) * 2 + c
+    n_mine = lax.dynamic_slice_in_dim(n_sum, me * cols, cols, 2)
+    return (
+        y_out,
+        x_grad,
+        both[:, 0, :, :width].reshape(w_qkv.shape),
+        both[:, 0, :, width:],
+        both[:, 1],
+        both[:, 2],
+        n_mine[:, :2],
+        n_mine[:, 2:4],
+    )
 
 
 def typed_map(operand, stacked, chain_kinds, pattern):
@@ -46,14 +477,14 @@
     return result.reshape(row_count, result.shape[-1])
 
 
-def norm_forward(values, gain_rows, shift_rows):
+def old_norm_forward(values, gain_rows, shift_rows):
     center = values - jnp.mean(values, -1, keepdims=True)
     factor = lax.rsqrt(jnp.mean(center * center, -1, keepdims=True) + EPS)
     normed = center * factor
     return (normed * gain_rows + shift_rows, normed, factor)
 
 
-def norm_backward(grad_out, normed, factor, gain_rows):
+def old_norm_backward(grad_out, normed, factor, gain_rows):
     scaled = grad_out * gain_rows
     mean_plain = jnp.mean(scaled, -1, keepdims=True)
     mean_normed = jnp.mean(scaled * normed, -1, keepdims=True)
@@ -64,7 +495,7 @@
     return jnp.dot(onehot.T, values, precision=HIGH, preferred_element_type=jnp.float32)
 
 
-def local(x_in, tags, lengths, w_qkv, w_out, w_up, w_down, norm_gain, norm_bias, cotangent):
+def general_local(x_in, tags, lengths, w_qkv, w_out, w_up, w_down, norm_gain, norm_bias, cotangent):
     tp_count = lax.axis_size("tensor")
     tp_index = lax.axis_index("tensor")
     local_rows = CHAINS_PART * LENGTH
@@ -148,7 +579,7 @@
             scatter_dimension=0,
             tiled=True,
         ).astype(jnp.float32)
-        mid, normed_mid, factor_mid = norm_forward(
+        mid, normed_mid, factor_mid = old_norm_forward(
             own_rows.astype(jnp.float32) + attn_sum, gain_mid, shift_mid
         )
         mid_all = lax.all_gather(mid.astype(jnp.bfloat16), "tensor", axis=0, tiled=True).reshape(
@@ -164,7 +595,7 @@
             scatter_dimension=0,
             tiled=True,
         ).astype(jnp.float32)
-        final, normed_end, factor_end = norm_forward(ffn_sum + mid, gain_end, shift_end)
+        final, normed_end, factor_end = old_norm_forward(ffn_sum + mid, gain_end, shift_end)
         outputs.append(final.astype(jnp.bfloat16))
         base = grad_full
         grad_final = cotangent[micro_index * local_rows : (micro_index + 1) * local_rows].astype(
@@ -172,7 +603,7 @@
         )
         gain_acc = gain_acc.at[:, 1].add(type_sums(onehot, grad_final * normed_end))
         shift_acc = shift_acc.at[:, 1].add(type_sums(onehot, grad_final))
-        grad_resid2 = norm_backward(grad_final, normed_end, factor_end, gain_end)
+        grad_resid2 = old_norm_backward(grad_final, normed_end, factor_end, gain_end)
         grad_ffn = lax.all_gather(
             grad_resid2.astype(jnp.bfloat16), "tensor", axis=0, tiled=True
         ).reshape(batch_chains, LENGTH, D)
@@ -191,7 +622,7 @@
         ).astype(jnp.float32)
         gain_acc = gain_acc.at[:, 0].add(type_sums(onehot, grad_mid * normed_mid))
         shift_acc = shift_acc.at[:, 0].add(type_sums(onehot, grad_mid))
-        grad_resid1 = norm_backward(grad_mid, normed_mid, factor_mid, gain_mid)
+        grad_resid1 = old_norm_backward(grad_mid, normed_mid, factor_mid, gain_mid)
         grad_attn = lax.all_gather(
             grad_resid1.astype(jnp.bfloat16), "tensor", axis=0, tiled=True
         ).reshape(batch_chains, LENGTH, D)
@@ -272,19 +703,35 @@
         P(None, None, ("dp", "tensor")),
         P(("dp", "tensor"), None),
     )
+    results = (
+        P(("dp", "tensor"), None),
+        P(("dp", "tensor"), None),
+        P(None, "dp", None, "tensor"),
+        P(None, "dp", "tensor"),
+        P(None, "dp", "tensor"),
+        P(None, "dp", "tensor"),
+        P(None, None, ("dp", "tensor")),
+        P(None, None, ("dp", "tensor")),
+    )
+    n_dp, n_tensor = mesh.shape["dp"], mesh.shape["tensor"]
+    if n_tensor != GROUPS or n_dp % 2 or D % (16 * n_dp):
+        return jax.shard_map(
+            general_local, mesh=mesh, in_specs=placed, out_specs=results, check_vma=False
+        )
+    fine = Mesh(mesh.devices.reshape(n_dp // 2, 2, 2, 2), AXES)
+    names = {"dp": ("z", "x"), "tensor": ("y", "c")}
+
+    def refine(spec):
+        parts = []
+        for entry in spec:
+            entry = (entry,) if isinstance(entry, str) else entry
+            parts.append(entry and sum((names[a] for a in entry), ()))
+        return P(*parts)
+
     return jax.shard_map(
-        local,
-        mesh=mesh,
-        in_specs=placed,
-        out_specs=(
-            P(("dp", "tensor"), None),
-            P(("dp", "tensor"), None),
-            P(None, "dp", None, "tensor"),
-            P(None, "dp", "tensor"),
-            P(None, "dp", "tensor"),
-            P(None, "dp", "tensor"),
-            P(None, None, ("dp", "tensor")),
-            P(None, None, ("dp", "tensor")),
-        ),
+        partial(split_local, n_dp // 2),
+        mesh=fine,
+        in_specs=tuple(refine(s) for s in placed),
+        out_specs=tuple(refine(s) for s in results),
         check_vma=False,
     )

time: 1830 us -> 511 us (0.28)
  loops' own time: 376 us -> 0 us
  matrix products: 479 us -> 152 us
  blocking collectives: 327 us -> 0 us
  local copies, waits for them, and re-layouts: 380 us -> 81 us
  Pallas kernels: 0 us -> 214 us
  waiting for transfers between devices: 85.6 us -> 0 us
  other arithmetic: 137 us -> 53.9 us
    another operation x48 -> x0, loops' own time: 376 us -> none  [the longest x32 250 us: typed_map(): return lax.map(single, (operand, chain_kinds))]
    dot_general x232 -> x18, matrix products: 479 us -> 152 us  [ein(): return jnp.einsum(pattern, *operands, preferred_element_type=F32)]
    all_gather x19 -> x0, blocking collectives: 285 us -> none  [the longest x4 44.9 us: local(): lax.all_gather(own_rows, 'tensor', axis=0, tiled=True)]
    dynamic_slice x257 -> x4, local copies, waits for them, and re-layouts: 240 us -> 0.3 us  [the longest x2 0.15 us: slots(): lent = lax.dynamic_slice_in_dim(values, (2 - y) * OWN + c * EXTRA, EXTRA)]
    pallas_call x0 -> x2, Pallas kernels: none -> 214 us  [the longest x1 118 us: gather_all(): pl.pallas_call(partial(gather_kernel, nz, rows), out_shape=(jax.ShapeDtyp...]
    reduce_scatter x20 -> x0, waiting for transfers between devices: 84.2 us -> none  [the longest x1 36.9 us: local(): lax.psum_scatter(grad_full[2], 'dp', scatter_dimension=1, tiled=True)]
    convert_element_type x20 -> x1, other arithmetic: 60.5 us -> 9.32 us  [layer(): (probs * (d_probs - jnp.sum(d_probs * probs, -1, keepdims=True))).astype(BF)]
    unnamed x1 -> x0, blocking collectives: 42.5 us -> none
  transfers between devices with their start and end apart: 23 -> 0, of which waited for: 4 -> 0; matrix products, arithmetic and copies ran while one was open for 45% -> 0% of each run, Pallas kernels for 0% -> 0%
where the time goes in v1:
time: 511 us; the launch traced here: 502 us
  Pallas kernels  214 us (42%)
  matrix products  152 us (30%)
  local copies, waits for them, and re-layouts  81 us (16%)
  other arithmetic  53.9 us (11%)
    dot_general x18, matrix products, ein(): return jnp.einsum(pattern, *operands, preferred_element_type=F32)  152 us
    pallas_call x1, Pallas kernels, gather_all(): pl.pallas_call(partial(gather_kernel, nz, rows), out_shape=(jax.ShapeDtyp...  118 us
    pallas_call x1, Pallas kernels, scatter_all(): pl.pallas_call(partial(scatter_kernel, nz, rows), out_shape=(jax.ShapeDty...  95.6 us
    reshape x1, local copies, waits for them, and re-layouts, layer(): jnp.stack([d_q, d_k, d_v], 3).reshape(GROUPS, ROWS, 3 * heads * HEAD_DIM)  14.3 us
    reshape x1, local copies, waits for them, and re-layouts, layer(): parts = proj.reshape(GROUPS, SLOTS, LENGTH, 3, heads, HEAD_DIM)  14.2 us
    another operation x2, other arithmetic, layer(): jnp.stack([jnp.concatenate([g_qkv, g_out], -1), g_up, g_down]).astype(BF)  14.1 us
    another operation x1, local copies, waits for them, and re-layouts, layer(): jnp.stack([d_q, d_k, d_v], 3).reshape(GROUPS, ROWS, 3 * heads * HEAD_DIM)  12.3 us
    sub x1, other arithmetic, layer(): probs = jax.nn.softmax(scores, axis=-1)  10.4 us

profile of v1, /device:TPU:5, one launch (start us, length us, event | category | flops | bytes accessed | tf_op | source)
XLA Modules:
  0.0 502.2 jit_solution(15487101470177300723)
XLA Ops:
  5.0 118.3 %gather_weights.1 = (bf16[3,4,768,768]{3,2,1,0:T(8,128)(2,1)}, bf16[320,768]{1,0:T(8,128)(2,1)}, bf16[320,768]{1,0:T(8,128)(2,1)}, f32[32,8,128]{2,1,0:T(8,128)}) custom-call(bf16[640,768]{1,0:T(8,128)(2,1)} %x_in.1, bf16[640,768]{1,0:T(8,128)(2,1)} %cot.1, bf16[2,96,768]{2,1,0:T(8,128)(2,1)} %pad_maximum_fusion.4.qo, bf16[2,96,768]{2,1,0:T(8,128)(2,1)} %up.1, ...), custom_call_target="tpu_custom_call" | custom-call | tf_op jit(solution)/shard_map/gather_weights/pallas_call | solution.py:162
  129.3 6.7 %convert_bitcast_fusion.2 = bf16[4,960,576]{1,2,0:T(8,128)(2,1)} fusion(bf16[4,768,768]{2,1,0:T(8,128)(2,1)S(1)} %slice_bitcast_fusion, bf16[960,768]{1,0:T(8,128)(2,1)S(1)} %constant_dynamic-update-slice_fusion), kind=kOutput, calls=%fused_computation.55 | convolution fusion | flops 3399598080 | bytes 9830400 | tf_op jit(solution)/shard_map/nd,tdk->tnk/dot_general | solution.py:351
  136.0 14.2 %reshape.116 = bf16[4,6,160,3,3,64]{2,1,5,4,3,0:T(8,128)(2,1)} reshape(bf16[4,960,576]{1,2,0:T(8,128)(2,1)} %convert_bitcast_fusion.2) | data formatting | bytes 8847360 | tf_op jit(solution)/shard_map/reshape | solution.py:360
  154.5 6.7 %fusion.65 = f32[4,6,3,160,160]{3,4,2,1,0:T(8,128)} fusion(bf16[4,6,160,1,3,64]{2,1,5,4,3,0:T(8,128)(2,1)S(1)} %get-tuple-element.65, bf16[4,6,160,1,3,64]{2,1,5,4,3,0:T(8,128)(2,1)S(1)} %get-tuple-element.64), kind=kOutput, calls=%fused_computation.108 | convolution fusion | flops 235929600 | bytes 10321920 | tf_op jit(solution)/shard_map/tcqhe,tckhe->tchqk/dot_general | solution.py:351
  161.5 10.4 %fusion.96 = (f32[4,6,3,160]{3,2,1,0:T(4,128)S(1)}, f32[4,6,3,160,160]{3,4,2,1,0:T(8,128)S(1)}) fusion(f32[4,6,3,160,160]{3,4,2,1,0:T(8,128)} %fusion.65, pred[6,160]{1,0:T(8,128)(4,1)S(1)} %iota_compare_fusion.1), kind=kOutput, calls=%fused_computation.170 | output fusion | flops 11059359 | bytes 14792640 | tf_op jit(solution)/shard_map/sub | solution.py:365
  182.0 4.9 fusion.97
  187.6 34.0 %fusion.10 = (bf16[4,960,768]{2,1,0:T(8,128)(2,1)S(1)}, f32[4,960,768]{2,1,0:T(8,128)}, f32[4,768,960]{1,2,0:T(8,128)}) fusion(bf16[3,4,768,768]{3,2,1,0:T(8,128)(2,1)} %get-tuple-element.17, f32[960,768]{1,0:T(8,128)S(1)} %get-tuple-element.77, f32[768]{0:T(1024)S(1)} %get-tuple-element.60, f32[768]{0:T(1024)S(1)} %get-tuple-element.61, ...), kind=kOutput, calls=%fused_computation.19 | convolution fusion | flops 4725227520 | bytes 37172736 | tf_op jit(solution)/shard_map/nd,tdf->tnf/dot_general | solution.py:351
  221.7 10.4 %fusion.98 = (f32[960]{0:T(1024)S(1)}, f32[960,768]{1,0:T(8,128)S(1)}) fusion(f32[768]{0:T(1024)S(1)} %get-tuple-element.60, f32[768]{0:T(1024)S(1)} %get-tuple-element.61, f32[960]{0:T(1024)S(1)} %add_rsqrt_fusion.1, f32[960,768]{1,0:T(8,128)} %copy-done.5, f32[960]{0:T(1024)S(1)} %broadcast_multiply_fusion.5, ...), kind=kOutput, calls=%fused_computation.172 | convolution fusion | flops 4534270976 | bytes 16532736 | tf_op jit(solution)/shard_map/tnf,tdf->nd/dot_general | solution.py:351
  233.4 4.8 multiply_reduce_fusion.1
  238.2 10.6 %convert_bitcast_fusion = bf16[1,4,768,768]{3,2,1,0:T(8,128)(2,1)} fusion(bf16[4,960,768]{2,1,0:T(8,128)(2,1)} %copy-done.31, f32[960,768]{1,0:T(8,128)S(1)} %get-tuple-element.80, f32[960]{0:T(1024)S(1)} %get-tuple-element.84, f32[960]{0:T(1024)S(1)} %get-tuple-element.85, f32[768]{0:T(1024)S(1)} %get-tuple-element.59, f32[960]{0:T(1024)S(1)} %add_rsqrt_fusion, ...), kind=kOutput, calls=%fused_computation.51 | convolution fusion | flops 4541792256 | bytes 15059904 | tf_op jit(solution)/shard_map/nd,tnf->tdf/dot_general | solution.py:351
  248.7 16.8 %fusion.7 = bf16[4,960,768]{2,1,0:T(8,128)(2,1)} fusion(f32[4,960,768]{2,1,0:T(8,128)} %get-tuple-element.63, f32[4,768,960]{1,2,0:T(8,128)} %get-tuple-element.78, bf16[3,4,768,768]{3,2,1,0:T(8,128)(2,1)} %get-tuple-element.17, f32[960,768]{1,0:T(8,128)S(1)} %get-tuple-element.80, f32[960]{0:T(1024)S(1)} %get-tuple-element.84, ...), kind=kOutput, calls=%fused_computation.11 | convolution fusion | flops 4580720640 | bytes 38652864 | tf_op jit(solution)/shard_map/nd,tdf->tnf/dot_general | solution.py:351
  265.6 10.3 %convert_bitcast_fusion.1 = bf16[1,4,768,768]{3,2,1,0:T(8,128)(2,1)} fusion(bf16[4,960,768]{2,1,0:T(8,128)(2,1)} %fusion.7, f32[960,768]{1,0:T(8,128)} %copy-done.5, f32[768]{0:T(1024)S(1)} %get-tuple-element.60, f32[768]{0:T(1024)S(1)} %get-tuple-element.61, f32[960]{0:T(1024)S(1)} %add_rsqrt_fusion.1, f32[960]{0:T(1024)S(1)} %broadcast_multiply_fusion.5), kind=kOutput, calls=%fused_computation.52 | convolution fusion | flops 4535894016 | bytes 13579776 | tf_op jit(solution)/shard_map/nd,tnf->tdf/dot_general | solution.py:351
  275.9 8.3 %multiply_reduce_fusion.2 = (f32[768]{0:T(1024)S(1)}, f32[960]{0:T(1024)S(1)}, f32[960]{0:T(1024)S(1)}, f32[768]{0:T(1024)S(1)}, f32[960,768]{1,0:T(8,128)S(1)}) fusion(f32[960,768]{1,0:T(8,128)S(1)} %copy-done.6, f32[960]{0:T(1024)S(1)} %add_rsqrt_fusion.1, f32[960]{0:T(1024)S(1)} %broadcast_multiply_fusion.5, f32[768]{0:T(1024)S(1)} %get-tuple-element.61, ...), kind=kOutput, calls=%fused_computation.70 | convolution fusion | flops 4546064384 | bytes 20982720 | tf_op jit(solution)/shard_map/tnf,tdf->nd/dot_general | solution.py:351
  290.6 4.9 fusion.68
  295.5 5.7 %reshape.119 = bf16[4,6,160,3,64]{2,1,4,3,0:T(8,128)(2,1)} reshape(bf16[4,960,192]{1,2,0:T(8,128)(2,1)} %fusion.68) | data formatting | bytes 2949120 | tf_op jit(solution)/shard_map/reshape | solution.py:391
  301.3 9.0 %convert_bitcast_fusion.3 = bf16[4,6,160,1,3,64]{2,5,4,1,0,3:T(8,128)(2,1)} fusion(bf16[4,6,160,3,64]{2,1,4,3,0:T(8,128)(2,1)} %reshape.119, f32[4,6,3,160,160]{3,4,2,1,0:T(8,128)} %copy-done.4, f32[4,6,3,160]{3,2,1,0:T(4,128)S(1)} %copy-done.25), kind=kOutput, calls=%fused_computation.103 | convolution fusion | flops 240353280 | bytes 10368000 | tf_op jit(solution)/shard_map/tchqk,tcqhe->tckhe/dot_general | solution.py:351
  310.3 10.2 %multiply_reduce_fusion = (f32[4,6,3,160]{3,2,1,0:T(4,128)S(1)}, f32[4,6,3,160,160]{3,4,2,1,0:T(8,128)}) fusion(f32[4,6,3,160,160]{3,4,2,1,0:T(8,128)S(1)} %bitcast.212, f32[4,6,3,160]{3,2,1,0:T(4,128)S(1)} %copy-done.25, bf16[4,6,160,1,3,64]{2,1,5,4,3,0:T(8,128)(2,1)} %copy-done.12, bf16[4,6,160,3,64]{2,1,4,3,0:T(8,128)(2,1)} %reshape.119), kind=kOutput, calls=%fused_computation.21 | convolution fusion | flops 241447680 | bytes 17786880 | tf_op jit(solution)/shard_map/tcqhe,tckhe->tchqk/dot_general | solution.py:351
  320.5 9.3 %multiply_convert_fusion = bf16[4,6,3,160,160]{3,4,2,1,0:T(8,128)(2,1)S(1)} fusion(f32[4,6,3,160,160]{3,4,2,1,0:T(8,128)} %get-tuple-element.83, f32[4,6,3,160]{3,2,1,0:T(4,128)S(1)} %get-tuple-element.82, f32[4,6,3,160,160]{3,4,2,1,0:T(8,128)} %copy-done.4, f32[4,6,3,160]{3,2,1,0:T(4,128)S(1)} %copy-done.25), kind=kLoop, calls=%fused_computation.20 | loop fusion | flops 7372800 | bytes 18524160 | tf_op jit(solution)/shard_map/convert_element_type | solution.py:393
  337.4 12.3 %copy.77 = bf16[4,6,160,3,3,64]{2,1,5,4,3,0:T(8,128)(2,1)} copy(bf16[4,6,160,3,3,64]{2,5,4,1,0,3:T(8,128)(2,1)} %pad_maximum_fusion.1) | data formatting | bytes 8847360 | tf_op jit(solution)/shard_map/stack | solution.py:397
  349.7 14.3 %reshape.120 = bf16[4,960,576]{1,2,0:T(8,128)(2,1)} reshape(bf16[4,6,160,3,3,64]{2,1,5,4,3,0:T(8,128)(2,1)} %copy.77) | data formatting | bytes 8847360 | tf_op jit(solution)/shard_map/reshape | solution.py:397
  364.1 7.7 %convolution_convert_fusion = bf16[4,576,768]{2,1,0:T(8,128)(2,1)} fusion(bf16[4,960,576]{1,2,0:T(8,128)(2,1)} %reshape.120, bf16[960,768]{1,0:T(8,128)(2,1)S(1)} %copy-done.20), kind=kOutput, calls=%fused_computation.97 | convolution fusion | flops 3399155712 | bytes 9437184 | tf_op jit(solution)/shard_map/nd,tnk->tdk/dot_general | solution.py:351
  371.7 6.3 %copy.78 = bf16[4,576,768]{1,2,0:T(8,128)(2,1)} copy(bf16[4,576,768]{2,1,0:T(8,128)(2,1)} %convolution_convert_fusion) | data formatting | bytes 7077888 | tf_op jit(solution)/shard_map/convert.12
  381.5 10.9 %pad_maximum_fusion.grads = bf16[3,4,768,768]{3,2,1,0:T(8,128)(2,1)} fusion(bf16[1,4,768,768]{3,2,1,0:T(8,128)(2,1)S(1)} %bitcast.215, bf16[1,4,768,768]{3,2,1,0:T(8,128)(2,1)} %convert_bitcast_fusion.1, bf16[1,4,768,768]{3,2,1,0:T(8,128)(2,1)S(1)} %maximum_bitcast_fusion), kind=kLoop, calls=%fused_computation.2 | loop fusion | flops 14155776 | bytes 28311552 | tf_op jit(solution)/shard_map/stack | solution.py:400
  398.1 95.6 %scatter_grads.1 = (f32[3,96,768]{2,1,0:T(8,128)S(1)}, bf16[3,96,768]{2,1,0:T(8,128)(2,1)S(1)}, f32[2,8,768]{2,1,0:T(8,128)S(1)}, bf16[640,768]{1,0:T(8,128)(2,1)S(1)}, bf16[640,768]{1,0:T(8,128)(2,1)S(1)}) custom-call(bf16[3,4,768,768]{3,2,1,0:T(8,128)(2,1)} %pad_maximum_fusion.grads, f32[8,768]{1,0:T(8,128)S(1)} %select_maximum_fusion.ngrad, ...), custom_call_target="tpu_custom_call" | custom-call | tf_op jit(solution)/shard_map/scatter_grads/pallas_call | solution.py:299
  (145 shorter events, 57.9 us)
Async XLA Ops:
  154.5 6.7 %copy-start = (bf16[4,6,160,1,3,64]{2,1,5,4,3,0:T(8,128)(2,1)}, bf16[4,6,160,1,3,64]{2,1,5,4,3,0:T(8,128)(2,1)S(1)}, u32[]{:S(2)}) copy-start(bf16[4,6,160,1,3,64]{2,1,5,4,3,0:T(8,128)(2,1)S(1)} %get-tuple-element.64) | copy-start | bytes 4423684
  154.5 6.7 %copy-start.2 = (bf16[4,6,160,1,3,64]{2,1,5,4,3,0:T(8,128)(2,1)}, bf16[4,6,160,1,3,64]{2,1,5,4,3,0:T(8,128)(2,1)S(1)}, u32[]{:S(2)}) copy-start(bf16[4,6,160,1,3,64]{2,1,5,4,3,0:T(8,128)(2,1)S(1)} %get-tuple-element.65) | copy-start | bytes 4423684
  154.5 17.5 %copy-start.12 = (bf16[4,6,160,1,3,64]{2,1,5,4,3,0:T(8,128)(2,1)}, bf16[4,6,160,1,3,64]{2,1,5,4,3,0:T(8,128)(2,1)S(1)}, u32[]{:S(2)}) copy-start(bf16[4,6,160,1,3,64]{2,1,5,4,3,0:T(8,128)(2,1)S(1)} %get-tuple-element.66) | copy-start | bytes 4423684
  154.5 6.7 %copy-start.28 = (s32[16]{0:T(128)S(1)}, s32[16]{0:T(128)}, u32[]{:S(2)}) copy-start(s32[16]{0:T(128)} %param.12) | copy-start | bytes 196
  186.9 34.8 %copy-start.5 = (f32[960,768]{1,0:T(8,128)}, f32[960,768]{1,0:T(8,128)S(1)}, u32[]{:S(2)}) copy-start(f32[960,768]{1,0:T(8,128)S(1)} %get-tuple-element.77) | copy-start | bytes 8847364
  221.7 10.4 %copy-start.31 = (bf16[4,960,768]{2,1,0:T(8,128)(2,1)}, bf16[4,960,768]{2,1,0:T(8,128)(2,1)S(1)}, u32[]{:S(2)}) copy-start(bf16[4,960,768]{2,1,0:T(8,128)(2,1)S(1)} %get-tuple-element.62) | copy-start | bytes 17694724
  221.7 10.9 %copy-start.29 = (s32[16]{0:T(128)S(1)}, s32[16]{0:T(128)}, u32[]{:S(2)}) copy-start(s32[16]{0:T(128)} %param.11) | copy-start | bytes 196
  265.5 10.3 %copy-start.6 = (f32[960,768]{1,0:T(8,128)S(1)}, f32[960,768]{1,0:T(8,128)}, u32[]{:S(2)}) copy-start(f32[960,768]{1,0:T(8,128)} %copy-done.5) | copy-start | bytes 8847364
  265.5 10.3 %copy-start.10 = (bf16[640,768]{1,0:T(8,128)(2,1)S(1)}, bf16[640,768]{1,0:T(8,128)(2,1)}, u32[]{:S(2)}) copy-start(bf16[640,768]{1,0:T(8,128)(2,1)} %cot.1) | copy-start | bytes 2949124
  265.6 10.3 %copy-start.30 = (bf16[4,960,768]{2,1,0:T(8,128)(2,1)S(1)}, bf16[4,960,768]{2,1,0:T(8,128)(2,1)}, u32[]{:S(2)}) copy-start(bf16[4,960,768]{2,1,0:T(8,128)(2,1)} %fusion.7) | copy-start | bytes 17694724
  295.5 5.8 %copy-start.25 = (f32[4,6,3,160]{3,2,1,0:T(4,128)S(1)}, f32[4,6,3,160]{3,2,1,0:T(4,128)}, u32[]{:S(2)}) copy-start(f32[4,6,3,160]{3,2,1,0:T(4,128)} %copy-done.24) | copy-start | bytes 138244
  295.5 14.8 %slice-start = ((s8[11796480]{0:T(1024)(128)(4,1)}), s8[3407872]{0:T(1024)(128)(4,1)S(1)}, s32[]{:S(2)}) async-start(s8[11796480]{0:T(1024)(128)(4,1)} %bitcast.211), calls=%async_computation | async-start | bytes 6815744
  301.3 9.0 %slice-start.1 = ((s8[11796480]{0:T(1024)(128)(4,1)}), s8[4194304]{0:T(1024)(128)(4,1)S(1)}, s32[]{:S(2)}) async-start(s8[11796480]{0:T(1024)(128)(4,1)} %bitcast.211), calls=%async_computation.1 | async-start | bytes 8388608
  301.3 9.0 %slice-start.2 = ((s8[11796480]{0:T(1024)(128)(4,1)}), s8[4194304]{0:T(1024)(128)(4,1)S(1)}, s32[]{:S(2)}) async-start(s8[11796480]{0:T(1024)(128)(4,1)} %bitcast.211), calls=%async_computation.2 | async-start | bytes 8388608
  320.5 9.3 %copy-start.3 = (bf16[4,6,160,1,3,64]{2,1,5,4,3,0:T(8,128)(2,1)S(1)}, bf16[4,6,160,1,3,64]{2,1,5,4,3,0:T(8,128)(2,1)}, u32[]{:S(2)}) copy-start(bf16[4,6,160,1,3,64]{2,1,5,4,3,0:T(8,128)(2,1)} %copy-done.2) | copy-start | bytes 4423684
  349.7 14.3 %copy-start.20 = (bf16[960,768]{1,0:T(8,128)(2,1)S(1)}, bf16[960,768]{1,0:T(8,128)(2,1)}, u32[]{:S(2)}) copy-start(bf16[960,768]{1,0:T(8,128)(2,1)} %copy-done.19) | copy-start | bytes 4423684
  371.7 6.3 %copy-start.7 = (bf16[4,192,768]{1,2,0:T(8,128)(2,1)S(1)}, bf16[4,192,768]{1,2,0:T(8,128)(2,1)}, u32[]{:S(2)}) copy-start(bf16[4,192,768]{1,2,0:T(8,128)(2,1)} %copy.79) | copy-start | bytes 3538948
  378.1 15.5 %slice-start.5 = ((s8[4718592]{0:T(1024)(128)(4,1)}), s8[4194304]{0:T(1024)(128)(4,1)S(1)}, s32[]{:S(2)}) async-start(s8[4718592]{0:T(1024)(128)(4,1)} %bitcast.216), calls=%async_computation.5 | async-start | bytes 8388608
  378.1 15.5 %slice-start.7 = ((s8[4718592]{0:T(1024)(128)(4,1)}), s8[524288]{0:T(1024)(128)(4,1)S(1)}, s32[]{:S(2)}) async-start(s8[4718592]{0:T(1024)(128)(4,1)} %bitcast.218), calls=%async_computation.7 | async-start | bytes 1048576
  381.5 12.1 %slice-start.6 = ((s8[4718592]{0:T(1024)(128)(4,1)}), s8[524288]{0:T(1024)(128)(4,1)S(1)}, s32[]{:S(2)}) async-start(s8[4718592]{0:T(1024)(128)(4,1)} %bitcast.216), calls=%async_computation.6 | async-start | bytes 1048576
  381.5 12.1 %slice-start.8 = ((s8[4718592]{0:T(1024)(128)(4,1)}), s8[4194304]{0:T(1024)(128)(4,1)S(1)}, s32[]{:S(2)}) async-start(s8[4718592]{0:T(1024)(128)(4,1)} %bitcast.218), calls=%async_computation.8 | async-start | bytes 8388608
  381.5 12.1 %copy-start.14 = (f32[960,768]{1,0:T(8,128)S(1)}, f32[960,768]{1,0:T(8,128)}, u32[]{:S(2)}) copy-start(f32[960,768]{1,0:T(8,128)} %copy-done.13) | copy-start | bytes 8847364
  398.0 95.7 %copy-start.16 = (f32[960,768]{1,0:T(8,128)}, f32[960,768]{1,0:T(8,128)S(1)}, u32[]{:S(2)}) copy-start(f32[960,768]{1,0:T(8,128)S(1)} %bitcast_add_fusion) | copy-start | bytes 8847364
  398.1 95.6 %copy-start.27 = (pred[6]{0:T(512)(128)(4,1)S(1)}, pred[6]{0:T(512)(128)(4,1)}, u32[]{:S(2)}) copy-start(pred[6]{0:T(512)(128)(4,1)} %copy-done.26) | copy-start | bytes 22
  (17 other events, 48.9 us)

commit v2 on v1

--- a/solution.py
+++ b/solution.py
@@ -333,73 +333,299 @@
     )(grads, ngrad, y_ext, g_ext)
 
 
-def norm_forward(values, gain, shift):
+CHUNK = 320
+N_CHUNK = ROWS // CHUNK
+WIDE = 3 * LENGTH
+GW = 256
+
+
+def dot_nn(a, b):
+    return lax.dot_general(a, b, (((1,), (0,)), ((), ())), preferred_element_type=F32)
+
+
+def dot_nt(a, b):
+    return lax.dot_general(a, b, (((1,), (1,)), ((), ())), preferred_element_type=F32)
+
+
+def dot_tn(a, b):
+    return lax.dot_general(a, b, (((0,), (0,)), ((), ())), preferred_element_type=F32)
+
+
+def lanes(shape):
+    return lax.broadcasted_iota(jnp.int32, shape, len(shape) - 1)
+
+
+def head_mask(h, shape):
+    lane = lanes(shape)
+    return jnp.logical_and(lane >= h * HEAD_DIM, lane < (h + 1) * HEAD_DIM)
+
+
+def stack_heads(rows):
+    zero = jnp.zeros_like(rows)
+    return jnp.concatenate([jnp.where(head_mask(h, rows.shape), rows, zero) for h in range(3)], 0)
+
+
+def merge_heads(stack):
+    out = jnp.zeros((LENGTH, GW), stack.dtype)
+    for h in range(3):
+        out = jnp.where(head_mask(h, out.shape), stack[h * LENGTH : (h + 1) * LENGTH], out)
+    return out
+
+
+def chunk_rows(i, size=CHUNK):
+    return pl.ds(pl.multiple_of(i * size, size), size)
+
+
+def loop(count, body):
+    def step(i, carry):
+        body(i)
+        return carry
+
+    lax.fori_loop(0, count, step, 0)
+
+
+def project(t, x, w, proj):
+    def rows(i):
+        r = chunk_rows(i)
+        proj[t, r] = dot_nn(x[r], w[0, t]).astype(BF)
+
+    loop(N_CHUNK, rows)
+
+
+def out_columns(t, w, wo):
+    low = lanes((D, 128)) < HEAD_DIM
+    tiles = [w[0, t, :, GW * i + 128 : GW * i + 256].astype(F32) for i in range(3)]
+    wo[t, :, :128] = jnp.where(low, pltpu.roll(tiles[0], 64, 1), tiles[1]).astype(BF)
+    wo[t, :, 128:] = jnp.where(low, pltpu.roll(tiles[2], 64, 1), 0.0).astype(BF)
+
+
+def attend(t, s, lens, proj, probs, hout):
+    r = chunk_rows(s, LENGTH)
+    query = stack_heads(proj[t, r, :GW] * jnp.asarray(0.125, BF))
+    scores = dot_nt(proj[t, r, GW : 2 * GW], query)
+    valid = lax.broadcasted_iota(jnp.int32, (LENGTH, 1), 0) < lens[s]
+    scores = jnp.where(valid, scores, NEG)
+    expo = jnp.exp(scores - jnp.max(scores, 0, keepdims=True))
+    low = (expo * (1.0 / jnp.sum(expo, 0, keepdims=True))).astype(BF)
+    probs[t, s, :, :WIDE] = low
+    hout[t, r] = merge_heads(dot_tn(low, proj[t, r, 2 * GW :])).astype(BF)
+
+
+def norm_rows(values):
     center = values - jnp.mean(values, -1, keepdims=True)
     factor = lax.rsqrt(jnp.mean(center * center, -1, keepdims=True) + EPS)
-    normed = center * factor
-    return normed * gain + shift, normed, factor
-
-
-def norm_backward(grad_out, normed, factor, gain):
-    scaled = grad_out * gain
-    mean_plain = jnp.mean(scaled, -1, keepdims=True)
-    mean_normed = jnp.mean(scaled * normed, -1, keepdims=True)
-    return factor * (scaled - mean_plain - normed * mean_normed)
-
-
-def ein(pattern, *operands):
-    return jnp.einsum(pattern, *operands, preferred_element_type=F32)
-
-
-def layer(x, cot, lens, w, gains, shifts):
-    heads = HEADS // GROUPS
-    qkv_w = w[0][:, :, : 3 * heads * HEAD_DIM]
-    out_w = w[0][:, :, 3 * heads * HEAD_DIM :]
-    up_w, down_w = w[1], w[2]
-    proj = ein("nd,tdk->tnk", x, qkv_w).astype(BF)
-    parts = proj.reshape(GROUPS, SLOTS, LENGTH, 3, heads, HEAD_DIM)
-    query, key, value = parts[:, :, :, 0], parts[:, :, :, 1], parts[:, :, :, 2]
-    valid = lax.broadcasted_iota(jnp.int32, (SLOTS, LENGTH), 1) < lens[:, None]
-    scores = ein("tcqhe,tckhe->tchqk", query, key) * 0.125
-    scores = jnp.where(valid[None, :, None, None, :], scores, NEG)
-    probs = jax.nn.softmax(scores, axis=-1)
-    low = probs.astype(BF)
-    hout = ein("tchqk,tckhe->tcqhe", low, value).astype(BF).reshape(GROUPS, ROWS, heads * HEAD_DIM)
-    attn = ein("tnh,tdh->nd", hout, out_w)
-    mid, n1, s1 = norm_forward(x.astype(F32) + attn, gains[0], shifts[0])
-    mid_low = mid.astype(BF)
-    up = ein("nd,tdf->tnf", mid_low, up_w)
-    act, pull = jax.vjp(partial(jax.nn.gelu, approximate=False), up)
-    act = act.astype(BF)
-    ffn = ein("tnf,tdf->nd", act, down_w)
-    final, n2, s2 = norm_forward(ffn + mid, gains[1], shifts[1])
-    y = final.astype(BF)
-    dr2 = norm_backward(cot, n2, s2, gains[1])
-    ngrad = [None, jnp.sum(cot * n2, 0), None, jnp.sum(cot, 0)]
-    d_ffn = dr2.astype(BF)
-    d_act = ein("nd,tdf->tnf", d_ffn, down_w)
-    d_up = pull(d_act)[0].astype(BF)
-    g_down = ein("nd,tnf->tdf", d_ffn, act)
-    g_up = ein("nd,tnf->tdf", mid_low, d_up)
-    d_mid = dr2 + ein("tnf,tdf->nd", d_up, up_w)
-    dr1 = norm_backward(d_mid, n1, s1, gains[0])
-    ngrad[0] = jnp.sum(d_mid * n1, 0)
-    ngrad[2] = jnp.sum(d_mid, 0)
-    d_attn = dr1.astype(BF)
-    d_heads = ein("nd,tdh->tnh", d_attn, out_w).astype(BF)
-    g_out = ein("nd,tnh->tdh", d_attn, hout)
-    d_heads = d_heads.reshape(GROUPS, SLOTS, LENGTH, heads, HEAD_DIM)
-    d_probs = ein("tcqhe,tckhe->tchqk", d_heads, value)
-    d_scores = (probs * (d_probs - jnp.sum(d_probs * probs, -1, keepdims=True))).astype(BF)
-    d_q = (ein("tchqk,tckhe->tcqhe", d_scores, key) * 0.125).astype(BF)
-    d_k = (ein("tchqk,tcqhe->tckhe", d_scores, query) * 0.125).astype(BF)
-    d_v = ein("tchqk,tcqhe->tckhe", low, d_heads).astype(BF)
-    d_proj = jnp.stack([d_q, d_k, d_v], 3).reshape(GROUPS, ROWS, 3 * heads * HEAD_DIM)
-    g_qkv = ein("nd,tnk->tdk", x, d_proj)
-    x_grad = dr1 + ein("tnk,tdk->nd", d_proj, qkv_w)
-    grads = jnp.stack([jnp.concatenate([g_qkv, g_out], -1), g_up, g_down]).astype(BF)
-    ngrad = jnp.pad(jnp.stack(ngrad), ((0, 4), (0, 0)))
-    return y, x_grad, grads, ngrad
+    return center * factor, factor
+
+
+def norm_back(scaled, normed, factor):
+    return factor * (
+        scaled
+        - jnp.mean(scaled, -1, keepdims=True)
+        - normed * jnp.mean(scaled * normed, -1, keepdims=True)
+    )
+
+
+def first_norm(i, x, hout, wo, prm, mid, n1, s1, mid_low):
+    r = chunk_rows(i)
+    attn = dot_nt(hout[0, r], wo[0])
+    for t in range(1, GROUPS):
+        attn += dot_nt(hout[t, r], wo[t])
+    normed, factor = norm_rows(x[r].astype(F32) + attn)
+    n1[r] = normed
+    s1[r] = jnp.broadcast_to(factor, (CHUNK, 128))
+    value = normed * prm[0:1] + prm[2:3]
+    mid[r] = value
+    mid_low[r] = value.astype(BF)
+
+
+def feed_up(t, i, mid_low, w, act, slope):
+    r = chunk_rows(i)
+    up = dot_nn(mid_low[r], w[1, t])
+    cdf = 0.5 * (1.0 + lax.erf(up * 0.7071067811865476))
+    act[t, r] = (up * cdf).astype(BF)
+    slope[t, r] = (cdf + up * (0.3989422804014327 * jnp.exp(-0.5 * up * up))).astype(BF)
+
+
+def second_norm(i, act, w, prm, mid, cot, mine, y_rows, d_ffn, ngrad):
+    r = chunk_rows(i)
+    ffn = dot_nt(act[0, r], w[2, 0])
+    for t in range(1, GROUPS):
+        ffn += dot_nt(act[t, r], w[2, t])
+    normed, factor = norm_rows(ffn + mid[r])
+    y_rows[r] = (normed * prm[1:2] + prm[3:4]).astype(BF)
+    first = lax.broadcasted_iota(jnp.int32, (CHUNK, 1), 0) < LENGTH
+    grad = cot[r].astype(F32) * jnp.where(first, mine[2 * i], mine[2 * i + 1])
+    ngrad[1:2] += jnp.sum(grad * normed, 0, keepdims=True)
+    ngrad[3:4] += jnp.sum(grad, 0, keepdims=True)
+    back = norm_back(grad * prm[1:2], normed, factor)
+    mid[r] = back
+    d_ffn[r] = back.astype(BF)
+
+
+def back_up(t, i, d_ffn, w, slope):
+    r = chunk_rows(i)
+    slope[t, r] = (dot_nn(d_ffn[r], w[2, t]) * slope[t, r].astype(F32)).astype(BF)
+
+
+def back_first_norm(i, d_up, w, prm, mid, n1, s1, d_attn, ngrad):
+    r = chunk_rows(i)
+    grad = mid[r]
+    for t in range(GROUPS):
+        grad += dot_nt(d_up[t, r], w[1, t])
+    ngrad[0:1] += jnp.sum(grad * n1[r], 0, keepdims=True)
+    ngrad[2:3] += jnp.sum(grad, 0, keepdims=True)
+    back = norm_back(grad * prm[0:1], n1[r], s1[r, 0:1])
+    mid[r] = back
+    d_attn[r] = back.astype(BF)
+
+
+def back_heads(t, i, d_attn, wo, d_heads):
+    r = chunk_rows(i)
+    d_heads[t, r, :GW] = dot_nn(d_attn[r], wo[t]).astype(BF)
+
+
+def back_attend(t, s, proj, probs, d_heads):
+    r = chunk_rows(s, LENGTH)
+    grad = stack_heads(d_heads[t, r, :GW])
+    low = probs[t, s, :, :WIDE]
+    p = low.astype(F32)
+    d_probs = dot_nt(proj[t, r, 2 * GW :], grad)
+    d_scores = (p * (d_probs - jnp.sum(d_probs * p, 0, keepdims=True))).astype(BF)
+    query = stack_heads(proj[t, r, :GW] * jnp.asarray(0.125, BF))
+    key = proj[t, r, GW : 2 * GW]
+    d_query = merge_heads(dot_tn(d_scores, key)) * 0.125
+    d_key = dot_nn(d_scores, query)
+    d_value = dot_nn(low, grad)
+    proj[t, r, :GW] = d_query.astype(BF)
+    proj[t, r, GW : 2 * GW] = d_key.astype(BF)
+    proj[t, r, 2 * GW :] = d_value.astype(BF)
+
+
+def grad_qkv_out(t, x, d_proj, d_attn, hout, store):
+    low = lanes((D, 128)) < HEAD_DIM
+    outs = dot_tn(d_attn[...], hout[t])
+    places = (pltpu.roll(outs[:, :128], 64, 1), outs[:, :128], pltpu.roll(outs[:, 128:], 64, 1))
+    for i in range(3):
+        part = dot_tn(x[...], d_proj[t, :, GW * i : GW * (i + 1)])
+        store(GW * i, part[:, :128])
+        store(GW * i + 128, jnp.where(low, part[:, 128:], places[i]))
+
+
+def back_input(i, d_proj, w, mid, out):
+    r = chunk_rows(i)
+    grad = mid[r]
+    for t in range(GROUPS):
+        grad += dot_nt(d_proj[t, r], w[0, t])
+    out(r, grad)
+
+
+def layer_kernel(x_hbm, cot_hbm, lens, mine, prm, w_hbm, y_rows, g_rows, grads, ngrad,
+                 w, x, cot, proj, probs, hout, wo, mid, n1, s1, mid_low, act, slope, d_ffn, slot, l_s, g_s):
+    loads = [pltpu.make_async_copy(x_hbm, x, l_s.at[3]), pltpu.make_async_copy(cot_hbm, cot, l_s.at[4])]
+    loads += [pltpu.make_async_copy(w_hbm.at[m], w.at[m], l_s.at[m]) for m in range(3)]
+    for cp in loads:
+        cp.start()
+    ngrad[...] = jnp.zeros_like(ngrad)
+    loads[0].wait()
+    loads[2].wait()
+
+    def one(t):
+        project(t, x, w, proj)
+        out_columns(t, w, wo)
+
+    loop(GROUPS, one)
+    loop(GROUPS * SLOTS, lambda i: attend(i // SLOTS, i % SLOTS, lens, proj, probs, hout))
+    loop(N_CHUNK, lambda i: first_norm(i, x, hout, wo, prm, mid, n1, s1, mid_low))
+    loads[3].wait()
+    loop(GROUPS * N_CHUNK, lambda i: feed_up(i // N_CHUNK, i % N_CHUNK, mid_low, w, act, slope))
+    loads[4].wait()
+    loads[1].wait()
+    loop(N_CHUNK, lambda i: second_norm(i, act, w, prm, mid, cot, mine, y_rows, d_ffn, ngrad))
+
+    def put(m, t, j):
+        return pltpu.make_async_copy(slot.at[j], grads.at[m, t], g_s.at[j])
+
+    def grad_loop(m, a, b):
+        def body(t):
+            j = t % 2
+
+            @pl.when(t >= 2)
+            def _():
+                put(m, t, j).wait()
+
+            slot[j] = dot_tn(a[...], b[t]).astype(BF)
+            put(m, t, j).start()
+
+        loop(GROUPS, body)
+        for j in range(2):
+            put(m, 0, j).wait()
+
+    grad_loop(2, d_ffn, act)
+    loop(GROUPS * N_CHUNK, lambda i: back_up(i // N_CHUNK, i % N_CHUNK, d_ffn, w, slope))
+    grad_loop(1, mid_low, slope)
+    loop(N_CHUNK, lambda i: back_first_norm(i, slope, w, prm, mid, n1, s1, d_ffn, ngrad))
+    loop(GROUPS * N_CHUNK, lambda i: back_heads(i // N_CHUNK, i % N_CHUNK, d_ffn, wo, act))
+    loop(GROUPS * SLOTS, lambda i: back_attend(i // SLOTS, i % SLOTS, proj, probs, act))
+
+    def last(t):
+        j = t % 2
+
+        @pl.when(t >= 2)
+        def _():
+            put(0, t, j).wait()
+
+        def store(col, value):
+            slot[j, :, pl.ds(col, 128)] = value.astype(BF)
+
+        grad_qkv_out(t, x, proj, d_ffn, hout, store)
+        put(0, t, j).start()
+
+    loop(GROUPS, last)
+    for j in range(2):
+        put(0, 0, j).wait()
+
+    def write(r, grad):
+        g_rows[r] = grad
+
+    loop(N_CHUNK, lambda i: back_input(i, proj, w, mid, write))
+
+
+def run_layer(x, cot, lens, mine, prm, w):
+    V = pl.BlockSpec(memory_space=pltpu.VMEM)
+    S = pl.BlockSpec(memory_space=pltpu.SMEM)
+    sem = pltpu.SemaphoreType.DMA
+    return pl.pallas_call(
+        layer_kernel,
+        out_shape=(
+            jax.ShapeDtypeStruct((ROWS, D), BF),
+            jax.ShapeDtypeStruct((ROWS, D), F32),
+            jax.ShapeDtypeStruct((3, GROUPS, D, D), BF),
+            jax.ShapeDtypeStruct((8, D), F32),
+        ),
+        in_specs=[ANY, ANY, S, S, V, ANY],
+        out_specs=(V, V, ANY, V),
+        scratch_shapes=[
+            pltpu.VMEM((3, GROUPS, D, D), BF),
+            pltpu.VMEM((ROWS, D), BF),
+            pltpu.VMEM((ROWS, D), BF),
+            pltpu.VMEM((GROUPS, ROWS, D), BF),
+            pltpu.VMEM((GROUPS, SLOTS, LENGTH, 512), BF),
+            pltpu.VMEM((GROUPS, ROWS, GW), BF),
+            pltpu.VMEM((GROUPS, D, GW), BF),
+            pltpu.VMEM((ROWS, D), F32),
+            pltpu.VMEM((ROWS, D), F32),
+            pltpu.VMEM((ROWS, 128), F32),
+            pltpu.VMEM((ROWS, D), BF),
+            pltpu.VMEM((GROUPS, ROWS, D), BF),
+            pltpu.VMEM((GROUPS, ROWS, D), BF),
+            pltpu.VMEM((ROWS, D), BF),
+            pltpu.VMEM((2, D, D), BF),
+            sem((5,)),
+            sem((2,)),
+        ],
+        compiler_params=pltpu.CompilerParams(vmem_limit_bytes=67043328),
+        name="layer",
+    )(x, cot, lens, mine, prm, w)
 
 
 def split_local(nz, x_in, tags, lengths, w_qkv, w_out, w_up, w_down, norm_gain, norm_bias, cotangent):
@@ -407,12 +633,15 @@
     rows = w_up.shape[1]
     cols = norm_gain.shape[2]
     own = 2 * y + c
-    qo = jnp.concatenate([w_qkv.reshape(2, rows, -1), w_out], -1)
+    qo = []
+    for i in range(3):
+        qo += [w_qkv[:, :, i], w_out[:, :, HEAD_DIM * i : HEAD_DIM * (i + 1)]]
+    qo = jnp.concatenate(qo, -1)
     norms = jnp.concatenate([norm_gain.reshape(4, cols), norm_bias.reshape(4, cols)], 0)
     norms = jnp.pad(norms, ((0, 0), (0, 128 - cols)))
     w, x_ext, cot_ext, n_all = gather_all(nz, x_in, cotangent, qo, w_up, w_down, norms)
     params = n_all[:, :, :cols].transpose(1, 0, 2).reshape(2, 2, 2, D)
-    params = lax.dynamic_index_in_dim(params, y, 1, keepdims=False)
+    params = lax.dynamic_index_in_dim(params, y, 1, keepdims=False).reshape(4, D)
 
     def slots(values):
         mine = lax.dynamic_slice_in_dim(values, own * OWN, OWN)
@@ -423,9 +652,10 @@
     lens = slots(lengths)
     mine = jnp.repeat(kinds == y, LENGTH)[:, None]
     rows_x = jnp.concatenate([x_in, x_ext])
-    rows_cot = jnp.concatenate([cotangent, cot_ext]).astype(F32)
-    rows_cot = jnp.where(mine, rows_cot, 0.0)
-    y_rows, g_rows, grads, ngrad = layer(rows_x, rows_cot, lens, w, params[0], params[1])
+    rows_cot = jnp.concatenate([cotangent, cot_ext])
+    y_rows, g_rows, grads, ngrad = run_layer(
+        rows_x, rows_cot, lens, (kinds == y).astype(F32), params, w
+    )
     own_g, oth_g, n_sum, y_back, g_back = scatter_all(
         nz, rows, grads, ngrad, y_rows[OWN_ROWS:], g_rows[OWN_ROWS:].astype(BF)
     )
@@ -433,14 +663,15 @@
     x_grad = jnp.where(mine[:OWN_ROWS], g_rows[:OWN_ROWS], g_back.astype(F32))
     oth_g = oth_g.astype(F32)
     both = jnp.stack([jnp.where(y == 0, own_g, oth_g), jnp.where(y == 0, oth_g, own_g)])
-    width = w_qkv.shape[2] * w_qkv.shape[3]
+    packed = both[:, 0].reshape(2, rows, 3, GW)
+    g_out = packed[..., GW - HEAD_DIM :].reshape(w_out.shape)
     me = ((z * 2 + x) * 2 + y) * 2 + c
     n_mine = lax.dynamic_slice_in_dim(n_sum, me * cols, cols, 2)
     return (
         y_out,
         x_grad,
-        both[:, 0, :, :width].reshape(w_qkv.shape),
-        both[:, 0, :, width:],
+        packed[..., : GW - HEAD_DIM],
+        g_out,
         both[:, 1],
         both[:, 2],
         n_mine[:, :2],

time: 511 us -> 349 us (0.68)
  matrix products: 152 us -> 0 us
  Pallas kernels: 214 us -> 319 us
  local copies, waits for them, and re-layouts: 81 us -> 13.1 us
  other arithmetic: 53.9 us -> 11.2 us
    dot_general x18 -> x0, matrix products: 152 us -> none  [ein(): return jnp.einsum(pattern, *operands, preferred_element_type=F32)]
    pallas_call x0 -> x1, Pallas kernels: none -> 105 us  [run_layer(): pl.pallas_call(layer_kernel, out_shape=(jax.ShapeDtypeStruct((ROWS, D), B...]
    reshape x5 -> x1, local copies, waits for them, and re-layouts: 38.3 us -> 0.62 us  [split_local(): lax.dynamic_index_in_dim(params, y, 1, keepdims=False).reshape(4, D)]
    another operation x7 -> x1, local copies, waits for them, and re-layouts: 21.1 us -> 0.31 us  [split_local(): packed = both[:, 0].reshape(2, rows, 3, GW)]
    another operation x4 -> x0, other arithmetic: 17.9 us -> none  [the longest x2 14.1 us: layer(): jnp.stack([jnp.concatenate([g_qkv, g_out], -1), g_up, g_down]).astype(BF)]
    sub x1 -> x0, other arithmetic: 10.4 us -> none  [layer(): probs = jax.nn.softmax(scores, axis=-1)]
    convert_element_type x1, other arithmetic: 9.32 us -> 0.59 us  [split_local(): (kinds == y).astype(F32)]
    unnamed x85 -> x12, local copies, waits for them, and re-layouts: 10 us -> 1.77 us
where the time goes in v2:
time: 349 us; the launch traced here: 344 us
  Pallas kernels  319 us (91%)
  local copies, waits for them, and re-layouts  13.1 us (4%)
  other arithmetic  11.2 us (3%)
    pallas_call x1, Pallas kernels, gather_all(): pl.pallas_call(partial(gather_kernel, nz, rows), out_shape=(jax.ShapeDtyp...  118 us
    pallas_call x1, Pallas kernels, run_layer(): pl.pallas_call(layer_kernel, out_shape=(jax.ShapeDtypeStruct((ROWS, D), B...  105 us
    pallas_call x1, Pallas kernels, scatter_all(): pl.pallas_call(partial(scatter_kernel, nz, rows), out_shape=(jax.ShapeDty...  95.6 us

profile of v2, /device:TPU:5, one launch (start us, length us, event | category | flops | bytes accessed | tf_op | source)
XLA Modules:
  0.0 344.1 jit_solution(13120807027397393125)
XLA Ops:
  0.6 0.7 dynamic_slice.20
  1.4 0.7 dynamic_slice.19
  2.1 0.6 fusion.6
  2.7 0.7 dynamic_slice.22
  3.4 0.7 dynamic_slice.21
  4.2 0.6 pad_add_fusion.lens
  4.7 1.0 slice_bitcast_fusion.1
  5.7 1.0 fusion.7
  6.7 0.9 concatenate.19.qo
  7.6 1.4 select_maximum_fusion.norms
  9.0 118.3 %gather_weights.1 = (bf16[3,4,768,768]{3,2,1,0:T(8,128)(2,1)}, bf16[320,768]{1,0:T(8,128)(2,1)}, bf16[320,768]{1,0:T(8,128)(2,1)}, f32[32,8,128]{2,1,0:T(8,128)}) custom-call(bf16[640,768]{1,0:T(8,128)(2,1)} %x_in.1, bf16[640,768]{1,0:T(8,128)(2,1)} %cot.1, bf16[2,96,768]{2,1,0:T(8,128)(2,1)} %concatenate.19.qo, bf16[2,96,768]{2,1,0:T(8,128)(2,1)} %up.1, ...), custom_call_target="tpu_custom_call" | custom-call | tf_op jit(solution)/shard_map/gather_weights/pallas_call | solution.py:162
  127.3 0.9 slice_bitcast_fusion
  128.4 0.6 reshape.37.prm
  129.1 3.0 pad_maximum_fusion
  132.1 105.1 %layer.1 = (bf16[960,768]{1,0:T(8,128)(2,1)}, f32[960,768]{1,0:T(8,128)}, bf16[3,4,768,768]{3,2,1,0:T(8,128)(2,1)}, f32[8,768]{1,0:T(8,128)}) custom-call(bf16[960,768]{1,0:T(8,128)(2,1)} %get-tuple-element.57.x_hbm, bf16[960,768]{1,0:T(8,128)(2,1)} %get-tuple-element.58.cot_hbm, s32[6]{0:T(128)} %pad_add_fusion.lens, f32[6]{0:T(128)} %get-tuple-element.42.mine, ...), custom_call_target="tpu_custom_call" | custom-call | tf_op jit(solution)/shard_map/layer/pallas_call | solution.py:597
  237.2 1.3 slice.108.g_ext
  238.5 1.1 slice.70.y_ext
  239.5 95.6 %scatter_grads.1 = (f32[3,96,768]{2,1,0:T(8,128)S(1)}, bf16[3,96,768]{2,1,0:T(8,128)(2,1)S(1)}, f32[2,8,768]{2,1,0:T(8,128)S(1)}, bf16[640,768]{1,0:T(8,128)(2,1)S(1)}, bf16[640,768]{1,0:T(8,128)(2,1)S(1)}) custom-call(bf16[3,4,768,768]{3,2,1,0:T(8,128)(2,1)} %get-tuple-element.26.grads, f32[8,768]{1,0:T(8,128)S(1)} %copy-done, ...), custom_call_target="tpu_custom_call" | custom-call | tf_op jit(solution)/shard_map/scatter_grads/pallas_call | solution.py:299
  335.3 1.1 fusion.5
  337.2 0.8 copy.28
  338.0 0.9 copy.27
  339.1 3.2 convert_select_fusion
  342.3 1.1 slice_select_fusion
  343.4 0.7 constant_dynamic-slice_fusion.1
  (19 shorter events, 1.2 us)
Async XLA Ops:
  7.6 121.5 %copy-start.1 = (bf16[640,768]{1,0:T(8,128)(2,1)S(1)}, bf16[640,768]{1,0:T(8,128)(2,1)}, u32[]{:S(2)}) copy-start(bf16[640,768]{1,0:T(8,128)(2,1)} %x_in.1) | copy-start | bytes 2949124
  7.6 121.5 %copy-start.2 = (bf16[640,768]{1,0:T(8,128)(2,1)S(1)}, bf16[640,768]{1,0:T(8,128)(2,1)}, u32[]{:S(2)}) copy-start(bf16[640,768]{1,0:T(8,128)(2,1)} %cot.1) | copy-start | bytes 2949124
  237.2 2.3 copy-start
  336.4 2.5 copy-start.4
  339.1 3.2 copy-start.3
